TPU v7x, 512 devices: a whole 4x4x16 slice. The times are simulated.
512 devices in a mesh: gx: 32 (over z, core), gy: 16 (over y, x).
Axes of the slice: x: 4, y: 4, z: 16, core: 2. Of those that a mesh axis runs over, the one named last changes fastest.
Arguments:
- field: float32 [1024, 512, 256], P('gx', 'gy'), may hold values from -192 to 192
- cond_x: float32 [1024, 512, 256], P('gx', 'gy'), may hold values from 1 to 4
- cond_y: float32 [1024, 512, 256], P('gx', 'gy'), may hold values from 1 to 4
- cross_weight: float32 [1024, 512, 256], P('gx', 'gy'), may hold values from -4 to 4
Outputs:
- field_next: float32 [1024, 512, 256], P('gx', 'gy')
All inputs are finite; a program needn't handle non-finite values.
Results may differ from a plain program's by a relative error of at most 0.0007.
Values sent between devices are 32-bit elements; how exact they have to be, the bound alone decides.
No kernel may reach another device: no remote copies, remote signals or barrier semaphores. Data moves between devices by JAX's collectives and lax.ppermute only.
A program may use at most 64 MiB of HBM per device.

v0:
```python
import functools

import jax
import jax.numpy as jnp
from jax import lax
from jax.experimental import pallas as pl
from jax.experimental.pallas import tpu as pltpu
from jax.sharding import PartitionSpec as P

STEP = 16384.0
LANES = 128
SUB = 8
VALUES = 5
MIB = 1 << 20
f32 = jnp.float32


def tile_view(x):
    nx, ny, nz = x.shape
    x = x.reshape(nx, ny // SUB, SUB, nz // LANES, LANES)
    return x.transpose(0, 1, 3, 2, 4).reshape(nx * ny * nz // LANES, LANES)


def from_tile_view(v, shape):
    nx, ny, nz = shape
    v = v.reshape(nx, ny // SUB, nz // LANES, SUB, LANES)
    return v.transpose(0, 1, 3, 2, 4).reshape(nx, ny, nz)


def y_rows(shape, y, half):
    nx, ny, nz = shape
    halves = nz // LANES
    start = ((y // SUB) * halves + half) * SUB + y % SUB
    return pl.ds(start, nx, stride=ny * halves)


def load_y(ref, shape, y):
    parts = [ref[y_rows(shape, y, h), :] for h in range(shape[2] // LANES)]
    return jnp.concatenate(parts, axis=1)


def store_y(ref, shape, y, value):
    for h in range(shape[2] // LANES):
        ref[y_rows(shape, y, h), :] = value[:, h * LANES : (h + 1) * LANES]


def store_plane(ref, shape, x, value):
    nx, ny, nz = shape
    halves = nz // LANES
    for yb in range(ny // SUB):
        for h in range(halves):
            start = ((x * (ny // SUB) + yb) * halves + h) * SUB
            ref[start : start + SUB, :] = value[
                yb * SUB : (yb + 1) * SUB, h * LANES : (h + 1) * LANES
            ]


def store_values(ref, values):
    lines, width = values[0].shape
    halves = width // LANES
    for k, value in enumerate(values):
        for h in range(halves):
            ref[pl.ds(k * halves + h, lines, stride=len(values) * halves), :] = value[
                :, h * LANES : (h + 1) * LANES
            ]


def load_values(ref, lines, count, halves):
    return [
        jnp.concatenate(
            [ref[pl.ds(k * halves + h, lines, stride=count * halves), :] for h in range(halves)],
            axis=1,
        )
        for k in range(count)
    ]


def eliminate(face, n, inv_ref, gam_ref, tau_ref, mat_ref):
    t = STEP * face(0)
    a = jnp.zeros_like(t)
    ground = jnp.ones_like(t)
    for i in range(n - 1):
        c = STEP * face(i + 1)
        inv = 1.0 / (t + ground + c)
        gam = c * inv
        tau = t * inv
        inv_ref[i] = inv
        gam_ref[i] = gam
        tau_ref[i] = tau
        a = a + tau * ground
        ground = 1.0 + gam * ground
        t = t * gam
    mat_ref[0] = t
    mat_ref[1] = a
    mat_ref[2] = ground


def matrix_x_kernel(c_ref, inv_ref, gam_ref, tau_ref, mat_ref):
    eliminate(lambda i: c_ref[i], c_ref.shape[0], inv_ref, gam_ref, tau_ref, mat_ref)


def matrix_y_kernel(shape, c_ref, inv_ref, gam_ref, tau_ref, mat_ref):
    eliminate(lambda y: load_y(c_ref, shape, y), shape[1], inv_ref, gam_ref, tau_ref, mat_ref)


def y_difference(plane, below, above):
    n = plane.shape[0]
    row = lax.broadcasted_iota(jnp.int32, plane.shape, 0)
    up = jnp.where(row == n - 1, above, pltpu.roll(plane, n - 1, 0))
    down = jnp.where(row == 0, below, pltpu.roll(plane, 1, 0))
    return up - down


def rim_kernel(first_ref, last_ref, below_ref, above_ref, d_first_ref, d_last_ref):
    n = below_ref.shape[0]
    d_first_ref[...] = y_difference(first_ref[0], below_ref[0:1, :], above_ref[0:1, :])
    d_last_ref[...] = y_difference(last_ref[0], below_ref[n - 1 : n, :], above_ref[n - 1 : n, :])


def forward(source, n, inv_ref, gam_ref, tau_ref, mat_ref, phi_ref, buf_ref):
    q = None
    j = None
    for i in range(n - 1):
        h = source(i) if q is None else source(i) + q
        phi_ref[i] = inv_ref[i] * h
        q = gam_ref[i] * h
        j = tau_ref[i] * h if j is None else j + tau_ref[i] * h
    q = q + source(n - 1)
    store_values(buf_ref, [mat_ref[0], mat_ref[1], mat_ref[2], j, q])


def backward(n, u_prev, u_own, gam_ref, tau_ref, phi_ref, emit):
    u = u_own
    emit(n - 1, u)
    for i in range(n - 2, -1, -1):
        u = phi_ref[i] + tau_ref[i] * u_prev + gam_ref[i] * u
        emit(i, u)


def forward_x_kernel(
    field_ref, weight_ref, below_ref, above_ref, dm_ref, dp_ref,
    inv_ref, gam_ref, tau_ref, mat_ref, phi_ref, buf_ref,
):
    n = field_ref.shape[0]

    def diff(i):
        if i < 0:
            return dm_ref[...]
        if i >= n:
            return dp_ref[...]
        return y_difference(field_ref[i], below_ref[i : i + 1, :], above_ref[i : i + 1, :])

    diffs = {}

    def source(i):
        for k in (i - 1, i, i + 1):
            if k not in diffs:
                diffs[k] = diff(k)
        mixed = diffs[i + 1] - diffs.pop(i - 1)
        return field_ref[i] + weight_ref[i] * mixed * 0.25

    forward(source, n, inv_ref, gam_ref, tau_ref, mat_ref, phi_ref, buf_ref)


def solve_kernel(n, m, halves, in_ref, out_ref):
    stride = m * VALUES * halves

    def get(k):
        return jnp.concatenate(
            [
                in_ref[pl.ds((l * VALUES + k) * halves + h, n, stride=stride), :]
                for l in range(m)
                for h in range(halves)
            ],
            axis=1,
        )

    t, a, ground, j, q = (get(k) for k in range(VALUES))
    row = lax.broadcasted_iota(jnp.int32, t.shape, 0)
    first = row == 0
    last = row == n - 1

    def after(v, d=1):
        return pltpu.roll(v, n - d, 0)

    def before(v, d=1):
        return pltpu.roll(v, d, 0)

    g = ground + jnp.where(last, 0.0, after(a)) + jnp.where(first, t, 0.0)
    low = jnp.where(first, 0.0, t)
    high = jnp.where(last, 0.0, after(t))
    r = q + jnp.where(last, 0.0, after(j))
    d = 1
    while d < n:
        inv = 1.0 / (g + low + high)
        gi = g * inv
        ri = r * inv
        g, r, low, high = (
            g + low * before(gi, d) + high * after(gi, d),
            r + low * before(ri, d) + high * after(ri, d),
            low * before(low * inv, d),
            high * after(high * inv, d),
        )
        d *= 2
    u = r / g
    u_prev = jnp.where(first, 0.0, before(u))
    for l in range(m):
        for k, value in enumerate((u_prev, u)):
            for h in range(halves):
                at = (l * halves + h) * LANES
                out_ref[pl.ds((l * 2 + k) * halves + h, n, stride=m * 2 * halves), :] = value[
                    :, at : at + LANES
                ]


def middle_kernel(
    shape, ends_ref, phi_x_ref, gam_x_ref, tau_x_ref, inv_ref, gam_ref, tau_ref, mat_ref,
    phi_ref, buf_ref, half_ref,
):
    nx, ny, nz = shape
    u_prev, u_own = load_values(ends_ref, ny, 2, nz // LANES)
    backward(nx, u_prev, u_own, gam_x_ref, tau_x_ref, phi_x_ref,
             lambda i, u: store_plane(half_ref, shape, i, u))
    forward(lambda y: load_y(half_ref, shape, y), ny, inv_ref, gam_ref, tau_ref, mat_ref, phi_ref, buf_ref)


def backward_y_kernel(shape, ends_ref, phi_ref, gam_ref, tau_ref, out_ref):
    nx, ny, nz = shape
    u_prev, u_own = load_values(ends_ref, nx, 2, nz // LANES)
    backward(ny, u_prev, u_own, gam_ref, tau_ref, phi_ref,
             lambda y, u: store_y(out_ref, shape, y, u))


def vmem(count):
    return [pl.BlockSpec(memory_space=pltpu.VMEM)] * count


def call(kernel, args, outs, name, scratch=(), cost=(1000, 1 << 20), in_specs=None):
    return pl.pallas_call(
        kernel,
        out_shape=[jax.ShapeDtypeStruct(s, f32) for s in outs],
        in_specs=vmem(len(args)) if in_specs is None else in_specs,
        out_specs=vmem(len(outs)),
        scratch_shapes=[pltpu.VMEM(s, f32) for s in scratch],
        compiler_params=pltpu.CompilerParams(vmem_limit_bytes=16 * MIB),
        cost_estimate=pl.CostEstimate(flops=cost[0], bytes_accessed=cost[1], transcendentals=0),
        name=name,
    )(*args)


def shift(value, axis, up):
    count = lax.axis_size(axis)
    pairs = [(i, i + 1) for i in range(count - 1)]
    return lax.ppermute(value, axis, pairs if up else [(j, i) for i, j in pairs])


def exchange(buf, axis):
    n = lax.axis_size(axis)
    rows, lanes = buf.shape
    got = lax.all_to_all(buf.reshape(n, 1, rows * lanes // n), axis, 0, 0, tiled=True)
    return got.reshape(rows, lanes)


def interfaces(buf, axis, lines, halves):
    n = lax.axis_size(axis)
    m = lines // n
    every = exchange(buf, axis)
    kernel = functools.partial(solve_kernel, n, m, halves)
    (ends,) = call(kernel, [every], [(n * m * 2 * halves, LANES)], "solve_" + axis)
    return exchange(ends, axis)


def shards(field, cond_x, cond_y, cross_weight):
    shape = nx, ny, nz = field.shape
    halves = nz // LANES
    below = shift(field[:, ny - 1, :], "gy", True)
    above = shift(field[:, 0, :], "gy", False)
    x_plane = (ny, nz)
    y_plane = (nx, nz)
    matrix_x = call(
        matrix_x_kernel, [cond_x], [(nx, *x_plane)] * 3 + [(3, *x_plane)], "matrix_x"
    )
    matrix_y = call(
        functools.partial(matrix_y_kernel, shape), [tile_view(cond_y)],
        [(ny, *y_plane)] * 3 + [(3, *y_plane)], "matrix_y",
    )
    d_first, d_last = call(
        rim_kernel, [field[:1], field[nx - 1 :], below, above], [x_plane] * 2, "rim"
    )
    d_before = shift(d_last, "gx", True)
    d_after = shift(d_first, "gx", False)
    phi_x, buf_x = call(
        forward_x_kernel,
        [field, cross_weight, below, above, d_before, d_after, *matrix_x],
        [(nx, *x_plane), (ny * VALUES * halves, LANES)],
        "forward_x",
    )
    ends_x = interfaces(buf_x, "gx", ny, halves)
    phi_y, buf_y = call(
        functools.partial(middle_kernel, shape),
        [ends_x, phi_x, matrix_x[1], matrix_x[2], *matrix_y],
        [(ny, *y_plane), (nx * VALUES * halves, LANES)],
        "middle",
        scratch=[(nx * ny * halves, LANES)],
    )
    ends_y = interfaces(buf_y, "gy", nx, halves)
    (out,) = call(
        functools.partial(backward_y_kernel, shape),
        [ends_y, phi_y, matrix_y[1], matrix_y[2]],
        [(nx * ny * halves, LANES)],
        "backward_y",
    )
    return from_tile_view(out, shape)


def solution(mesh):
    spec = P("gx", "gy", None)
    return jax.shard_map(
        shards, mesh=mesh, in_specs=(spec,) * 4, out_specs=spec, check_vma=False
    )
```

profile of v0, /device:TPU:2, one launch (start us, length us, event | category | flops | bytes accessed | tf_op | source)
XLA Modules:
  0.0 107.6 jit_solution(9846570008003693354)
XLA Ops:
  0.0 0.0 copy-start.3
  0.0 1.2 %fusion.1 = (f32[32,1,256]{2,1,0:T(1,128)S(1)}, f32[32,1,256]{2,1,0:T(1,128)S(1)}) fusion(f32[32,32,256]{2,1,0:T(8,128)} %field_ref.1), kind=kLoop, calls=%fused_computation.3 | loop fusion | bytes 131072 | tf_op jit(solution)/shard_map/slice | solution.py:277
  1.2 3.4 %collective-permute-start = (f32[32,256]{1,0:T(8,128)S(1)}, f32[32,256]{1,0:T(8,128)S(1)}, u32[]{:S(2)}, u32[]{:S(2)}) collective-permute-start(f32[32,256]{1,0:T(8,128)S(1)} %bitcast.32), channel_id=1, source_target_pairs={{0,1},{1,2},{2,3},{3,4},{4,5},{5,6},{6,7},{7,8},{8,9},{9,10},{10,1... | collective-permute-start | bytes 98312 | tf_op jit(solution)/shard_map/ppermute | solution.py:254
  4.6 5.7 %collective-permute-start.1 = (f32[32,256]{1,0:T(8,128)S(1)}, f32[32,256]{1,0:T(8,128)S(1)}, u32[]{:S(2)}, u32[]{:S(2)}) collective-permute-start(f32[32,256]{1,0:T(8,128)S(1)} %bitcast.33), channel_id=1, source_target_pairs={{1,0},{2,1},{3,2},{4,3},{5,4},{6,5},{7,6},{8,7},{9,8},{10,9},{11,1... | collective-permute-start | bytes 98312 | tf_op jit(solution)/shard_map/ppermute | solution.py:254
  10.3 0.8 fusion
  11.1 0.0 collective-permute-done.below_ref
  11.1 0.8 collective-permute-done.1.above_ref
  11.9 1.3 %collective-permute-start.2 = (f32[32,256]{1,0:T(8,128)S(1)}, f32[32,256]{1,0:T(8,128)S(1)}, u32[]{:S(2)}, u32[]{:S(2)}) collective-permute-start(f32[32,256]{1,0:T(8,128)S(1)} %get-tuple-element.19), channel_id=1, source_target_pairs={{0,16},{16,32},{32,48},{48,64},{64,80},{80,96},{96,112},{112,128},... | collective-permute-start | bytes 98312 | tf_op jit(solution)/shard_map/ppermute | solution.py:254
  13.2 1.3 %collective-permute-start.3 = (f32[32,256]{1,0:T(8,128)S(1)}, f32[32,256]{1,0:T(8,128)S(1)}, u32[]{:S(2)}, u32[]{:S(2)}) collective-permute-start(f32[32,256]{1,0:T(8,128)S(1)} %get-tuple-element.20), channel_id=1, source_target_pairs={{16,0},{32,16},{48,32},{64,48},{80,64},{96,80},{112,96},{128,112},... | collective-permute-start | bytes 98312 | tf_op jit(solution)/shard_map/ppermute | solution.py:254
  14.5 0.0 copy-start.8
  14.5 1.2 %copy-done.8 = f32[32,32,256]{2,1,0:T(8,128)S(1)} copy-done((f32[32,32,256]{2,1,0:T(8,128)S(1)}, f32[32,32,256]{2,1,0:T(8,128)}, u32[]{:S(2)}) %copy-start.8) | copy-done | bytes 1048600
  15.7 0.5 matrix_x.1
  16.2 0.0 collective-permute-done.2.dm_ref
  16.2 0.8 collective-permute-done.3.dp_ref
  17.0 0.0 copy-done.3
  17.0 0.0 copy-start.10
  17.0 1.2 %copy-done.10 = f32[32,32,256]{2,1,0:T(8,128)S(1)} copy-done((f32[32,32,256]{2,1,0:T(8,128)S(1)}, f32[32,32,256]{2,1,0:T(8,128)}, u32[]{:S(2)}) %copy-start.10) | copy-done | bytes 1048600
  18.2 0.5 forward_x.1
  18.7 0.0 copy-start.4
  18.7 1.0 copy-done.4
  19.7 36.0 %all_to_all.20 = f32[32,1,1280]{2,1,0:T(1,128)S(1)} all-to-all(f32[32,1,1280]{2,1,0:T(1,128)S(1)} %bitcast.30), channel_id=1, replica_groups=mesh['gx'=32,'gy'=16] {'gx'}, dimensions={0} | all-to-all | bytes 327680 | tf_op jit(solution)/shard_map/all_to_all | solution.py:260
  55.7 0.8 solve_gx.1
  56.4 3.8 %all-to-all-start.1 = ((f32[32,1,512]{2,1,0:T(1,128)}), f32[32,1,512]{2,1,0:T(1,128)S(1)}, u32[]{:S(2)}, u32[]{:S(2)}) async-start(f32[32,1,512]{2,1,0:T(1,128)} %bitcast.4), calls=%async_computation.1 | async-start | bytes 131072 | tf_op jit(solution)/shard_map/all_to_all | solution.py:260
  60.3 0.0 copy-start.9
  60.3 1.2 %copy-done.9 = f32[32,32,256]{2,1,0:T(8,128)S(1)} copy-done((f32[32,32,256]{2,1,0:T(8,128)S(1)}, f32[32,32,256]{2,1,0:T(8,128)}, u32[]{:S(2)}) %copy-start.9) | copy-done | bytes 1048600
  61.5 0.7 matrix_y.1
  62.2 0.0 copy-start
  62.2 1.0 copy-done
  63.2 0.0 copy-start.6
  63.2 1.0 copy-done.6
  64.2 10.4 %all-to-all-done.1 = f32[32,1,512]{2,1,0:T(1,128)S(1)} async-done(((f32[32,1,512]{2,1,0:T(1,128)}), f32[32,1,512]{2,1,0:T(1,128)S(1)}, u32[]{:S(2)}, u32[]{:S(2)}) %all-to-all-start.1) | async-done | bytes 65568 | tf_op jit(solution)/shard_map/all_to_all | solution.py:260
  74.6 0.0 copy-start.1
  74.6 1.2 %copy-done.1 = f32[32,32,256]{2,1,0:T(8,128)S(1)} copy-done((f32[32,32,256]{2,1,0:T(8,128)S(1)}, f32[32,32,256]{2,1,0:T(8,128)}, u32[]{:S(2)}) %copy-start.1) | copy-done | bytes 1048600
  75.9 0.0 copy-start.5
  75.9 1.2 %copy-done.5 = f32[32,32,256]{2,1,0:T(8,128)S(1)} copy-done((f32[32,32,256]{2,1,0:T(8,128)S(1)}, f32[32,32,256]{2,1,0:T(8,128)}, u32[]{:S(2)}) %copy-start.5) | copy-done | bytes 1048600
  77.1 0.0 copy-start.7
  77.1 1.2 %copy-done.7 = f32[32,32,256]{2,1,0:T(8,128)S(1)} copy-done((f32[32,32,256]{2,1,0:T(8,128)S(1)}, f32[32,32,256]{2,1,0:T(8,128)}, u32[]{:S(2)}) %copy-start.7) | copy-done | bytes 1048600
  78.3 0.0 copy-start.2
  78.3 0.8 middle.1
  79.1 15.6 %all_to_all.21 = f32[16,1,2560]{2,1,0:T(1,128)S(1)} all-to-all(f32[16,1,2560]{2,1,0:T(1,128)S(1)} %bitcast.31), channel_id=1, replica_groups=mesh['gx'=32,'gy'=16] {'gy'}, dimensions={0} | all-to-all | bytes 327680 | tf_op jit(solution)/shard_map/all_to_all | solution.py:260
  94.8 0.1 solve_gy.1
  94.9 10.7 %all_to_all.22 = f32[16,1,1024]{2,1,0:T(1,128)S(1)} all-to-all(f32[16,1,1024]{2,1,0:T(1,128)S(1)} %bitcast.29), channel_id=1, replica_groups=mesh['gx'=32,'gy'=16] {'gy'}, dimensions={0} | all-to-all | bytes 131072 | tf_op jit(solution)/shard_map/all_to_all | solution.py:260
  105.6 0.0 copy-done.2
  105.6 2.0 %backward_y.1 = f32[2048,128]{1,0:T(8,128)} custom-call(f32[128,128]{1,0:T(8,128)S(1)} %bitcast.28, f32[32,32,256]{2,1,0:T(8,128)S(1)} %get-tuple-element.32.phi_ref, f32[32,32,256]{2,1,0:T(8,128)S(1)} %get-tuple-element.28.gam_ref, f32[32,32,256]{2,1,0:T(8,128)S(1)} %copy-done.2), custom_call_target="tpu_custom_call" | custom-call | flops 1000 | bytes 1048576 | tf_op jit(solution)/shard_map/backward_y/pallas_call | solution.py:239
  (3 shorter events, 0.0 us)
Async XLA Ops:
  0.0 17.0 %copy-start.3 = (f32[32,32,256]{2,1,0:T(8,128)S(1)}, f32[32,32,256]{2,1,0:T(8,128)}, u32[]{:S(2)}) copy-start(f32[32,32,256]{2,1,0:T(8,128)} %field_ref.1) | copy-start | bytes 3145732
  1.2 9.9 %collective-permute-start = (f32[32,256]{1,0:T(8,128)S(1)}, f32[32,256]{1,0:T(8,128)S(1)}, u32[]{:S(2)}, u32[]{:S(2)}) collective-permute-start(f32[32,256]{1,0:T(8,128)S(1)} %bitcast.32), channel_id=1, source_target_pairs={{0,1},{1,2},{2,3},{3,4},{4,5},{5,6},{6,7},{7,8},{8,9},{9,10},{10,1... | collective-permute-start | bytes 98312 | tf_op jit(solution)/shard_map/ppermute | solution.py:254
  4.6 7.3 %collective-permute-start.1 = (f32[32,256]{1,0:T(8,128)S(1)}, f32[32,256]{1,0:T(8,128)S(1)}, u32[]{:S(2)}, u32[]{:S(2)}) collective-permute-start(f32[32,256]{1,0:T(8,128)S(1)} %bitcast.33), channel_id=1, source_target_pairs={{1,0},{2,1},{3,2},{4,3},{5,4},{6,5},{7,6},{8,7},{9,8},{10,9},{11,1... | collective-permute-start | bytes 98312 | tf_op jit(solution)/shard_map/ppermute | solution.py:254
  11.9 4.3 %collective-permute-start.2 = (f32[32,256]{1,0:T(8,128)S(1)}, f32[32,256]{1,0:T(8,128)S(1)}, u32[]{:S(2)}, u32[]{:S(2)}) collective-permute-start(f32[32,256]{1,0:T(8,128)S(1)} %get-tuple-element.19), channel_id=1, source_target_pairs={{0,16},{16,32},{32,48},{48,64},{64,80},{80,96},{96,112},{112,128},... | collective-permute-start | bytes 98312 | tf_op jit(solution)/shard_map/ppermute | solution.py:254
  13.2 3.8 %collective-permute-start.3 = (f32[32,256]{1,0:T(8,128)S(1)}, f32[32,256]{1,0:T(8,128)S(1)}, u32[]{:S(2)}, u32[]{:S(2)}) collective-permute-start(f32[32,256]{1,0:T(8,128)S(1)} %get-tuple-element.20), channel_id=1, source_target_pairs={{16,0},{32,16},{48,32},{64,48},{80,64},{96,80},{112,96},{128,112},... | collective-permute-start | bytes 98312 | tf_op jit(solution)/shard_map/ppermute | solution.py:254
  14.5 1.2 %copy-start.8 = (f32[32,32,256]{2,1,0:T(8,128)S(1)}, f32[32,32,256]{2,1,0:T(8,128)}, u32[]{:S(2)}) copy-start(f32[32,32,256]{2,1,0:T(8,128)} %c_ref.1) | copy-start | bytes 3145732
  17.0 1.2 %copy-start.10 = (f32[32,32,256]{2,1,0:T(8,128)S(1)}, f32[32,32,256]{2,1,0:T(8,128)}, u32[]{:S(2)}) copy-start(f32[32,32,256]{2,1,0:T(8,128)} %weight_ref.1) | copy-start | bytes 3145732
  18.7 1.0 copy-start.4
  56.4 18.2 %all-to-all-start.1 = ((f32[32,1,512]{2,1,0:T(1,128)}), f32[32,1,512]{2,1,0:T(1,128)S(1)}, u32[]{:S(2)}, u32[]{:S(2)}) async-start(f32[32,1,512]{2,1,0:T(1,128)} %bitcast.4), calls=%async_computation.1 | async-start | bytes 131072 | tf_op jit(solution)/shard_map/all_to_all | solution.py:260
  60.3 1.2 %copy-start.9 = (f32[32,32,256]{2,1,0:T(8,128)S(1)}, f32[32,32,256]{2,1,0:T(8,128)}, u32[]{:S(2)}) copy-start(f32[32,32,256]{2,1,0:T(8,128)} %param.6) | copy-start | bytes 3145732
  62.2 1.0 copy-start
  63.2 1.0 copy-start.6
  74.6 1.2 %copy-start.1 = (f32[32,32,256]{2,1,0:T(8,128)S(1)}, f32[32,32,256]{2,1,0:T(8,128)}, u32[]{:S(2)}) copy-start(f32[32,32,256]{2,1,0:T(8,128)} %copy-done) | copy-start | bytes 3145732
  75.9 1.2 %copy-start.5 = (f32[32,32,256]{2,1,0:T(8,128)S(1)}, f32[32,32,256]{2,1,0:T(8,128)}, u32[]{:S(2)}) copy-start(f32[32,32,256]{2,1,0:T(8,128)} %copy-done.4) | copy-start | bytes 3145732
  77.1 1.2 %copy-start.7 = (f32[32,32,256]{2,1,0:T(8,128)S(1)}, f32[32,32,256]{2,1,0:T(8,128)}, u32[]{:S(2)}) copy-start(f32[32,32,256]{2,1,0:T(8,128)} %copy-done.6) | copy-start | bytes 3145732
  78.3 27.3 %copy-start.2 = (f32[32,32,256]{2,1,0:T(8,128)S(1)}, f32[32,32,256]{2,1,0:T(8,128)}, u32[]{:S(2)}) copy-start(f32[32,32,256]{2,1,0:T(8,128)} %copy-done) | copy-start | bytes 3145732
where the time goes:
time: 108 us
  blocking collectives  62.3 us (58%)
  starting transfers between devices  15.5 us (14%)
  local copies, waits for them, and re-layouts  12.2 us (11%)
  waiting for transfers between devices  12 us (11%)
  Pallas kernels  5.49 us (5%)
    all_to_all x3, blocking collectives, exchange(): lax.all_to_all(buf.reshape(n, 1, rows * lanes // n), axis, 0, 0, tiled=True)  62.3 us
    ppermute x4, starting transfers between devices, shift(): lax.ppermute(value, axis, pairs if up else [(j, i) for i, j in pairs])  11.7 us
    all_to_all x1, waiting for transfers between devices, exchange(): lax.all_to_all(buf.reshape(n, 1, rows * lanes // n), axis, 0, 0, tiled=True)  10.4 us
    unnamed x24, local copies, waits for them, and re-layouts  10.3 us
    pallas_call x8, Pallas kernels, call(): pl.pallas_call(kernel, out_shape=[jax.ShapeDtypeStruct(s, f32) for s in o...  5.49 us
    all_to_all x1, starting transfers between devices, exchange(): lax.all_to_all(buf.reshape(n, 1, rows * lanes // n), axis, 0, 0, tiled=True)  3.84 us
  transfers between devices with their start and end apart: 5, of which 3 were waited for; matrix products, arithmetic and copies ran while one was open for 1% of the time, Pallas kernels for 1%

commit v1 on v0

v1 whole, which is shorter than its diff:
```python
import functools

import jax
import jax.numpy as jnp
from jax import lax
from jax.experimental import pallas as pl
from jax.experimental.pallas import tpu as pltpu
from jax.sharding import PartitionSpec as P

STEP = 16384.0
LANES = 128
SUB = 8
MIB = 1 << 20
f32 = jnp.float32


def tile_rows(x):
    nx, ny, nz = x.shape
    x = x.reshape(nx, ny // SUB, SUB, nz // LANES, LANES)
    return x.transpose(0, 1, 3, 2, 4).reshape(nx * ny * nz // LANES, LANES)


def from_y_blocks(v, shape):
    nx, ny, nz = shape
    v = v.reshape(nx, ny // SUB, nz // LANES, SUB, LANES)
    return v.transpose(0, 1, 3, 2, 4).reshape(nx, ny, nz)


def y_scratch(shape):
    nx, ny, nz = shape
    return pltpu.VMEM((ny // SUB, nx * nz * SUB // LANES, LANES), f32)


def y_rows(shape, y, h):
    nx, _, nz = shape
    return y // SUB, pl.ds(h * SUB + y % SUB, nx, stride=SUB * nz // LANES), slice(None)


def load_y(ref, shape, y):
    return jnp.concatenate([ref[y_rows(shape, y, h)] for h in range(shape[2] // LANES)], axis=1)


def load_y_whole(ref, shape, y):
    nx, ny, nz = shape
    at = y // SUB * SUB * (nz // LANES) + y % SUB
    parts = [
        ref[pl.ds(at + h * SUB, nx, stride=ny * nz // LANES), :] for h in range(nz // LANES)
    ]
    return jnp.concatenate(parts, axis=1)


def store_y(ref, shape, y, value):
    for h in range(shape[2] // LANES):
        ref[y_rows(shape, y, h)] = value[:, h * LANES : (h + 1) * LANES]


def store_plane(ref, shape, x, value):
    _, ny, nz = shape
    halves = nz // LANES
    for yb in range(ny // SUB):
        for h in range(halves):
            start = (x * halves + h) * SUB
            ref[yb, start : start + SUB, :] = value[
                yb * SUB : (yb + 1) * SUB, h * LANES : (h + 1) * LANES
            ]


def y_block_out(scratch, hbm, yb, sem):
    block = scratch.at[yb].reshape(hbm.shape[0], hbm.shape[2], LANES)
    return pltpu.make_async_copy(block, hbm.at[:, yb], sem.at[yb])


def store_values(ref, values):
    lines, width = values[0].shape
    halves = width // LANES
    for k, value in enumerate(values):
        for h in range(halves):
            ref[pl.ds(k * halves + h, lines, stride=len(values) * halves), :] = value[
                :, h * LANES : (h + 1) * LANES
            ]


def load_values(ref, lines, count, halves):
    return [
        jnp.concatenate(
            [ref[pl.ds(k * halves + h, lines, stride=count * halves), :] for h in range(halves)],
            axis=1,
        )
        for k in range(count)
    ]


def matrix_x_kernel(c_ref, inv_ref, gam_ref, tau_ref, mat_ref):
    n = c_ref.shape[0]
    left = STEP * c_ref[0]
    t = left
    a = jnp.zeros_like(t)
    ground = jnp.ones_like(t)
    for i in range(n - 1):
        c = STEP * c_ref[i + 1]
        inv = 1.0 / (t + ground + c)
        gam = c * inv
        tau = t * inv
        inv_ref[i] = inv
        gam_ref[i] = gam
        tau_ref[i] = tau
        a = a + tau * ground
        ground = 1.0 + gam * ground
        t = t * gam
    for k, value in enumerate((t, a, ground, left)):
        mat_ref[k] = value


def y_difference(plane, below, above):
    n = plane.shape[0]
    row = lax.broadcasted_iota(jnp.int32, plane.shape, 0)
    up = jnp.where(row == n - 1, above, pltpu.roll(plane, n - 1, 0))
    down = jnp.where(row == 0, below, pltpu.roll(plane, 1, 0))
    return up - down


def rim_kernel(field_ref, below_ref, above_ref, mat_ref, up_ref, down_ref):
    n = field_ref.shape[0]
    ny = field_ref.shape[1]
    up_ref[...] = y_difference(field_ref[n - 1], below_ref[n - 1 : n, :], above_ref[n - 1 : n, :])
    down_ref[0:ny, :] = y_difference(field_ref[0], below_ref[0:1, :], above_ref[0:1, :])
    down_ref[ny:, :] = mat_ref[1]


def forward_x_kernel(
    field_ref, weight_ref, below_ref, above_ref, inv_ref, gam_ref, tau_ref, phi_ref, side_ref,
):
    n = field_ref.shape[0]
    diffs = {}

    def diff(i):
        if not 0 <= i < n:
            return 0.0
        if i not in diffs:
            diffs[i] = y_difference(field_ref[i], below_ref[i : i + 1, :], above_ref[i : i + 1, :])
        return diffs[i]

    q = j = 0.0
    for i in range(n):
        mixed = diff(i + 1) - diff(i - 1)
        diffs.pop(i - 1, None)
        h = field_ref[i] + weight_ref[i] * mixed * 0.25 + q
        if i < n - 1:
            phi_ref[i] = inv_ref[i] * h
            q = gam_ref[i] * h
            j = j + tau_ref[i] * h
    for k, value in enumerate((j, h, weight_ref[0] * 0.25, weight_ref[n - 1] * 0.25)):
        side_ref[k] = value


def finish_x_kernel(before_ref, after_ref, mat_ref, side_ref, buf_ref, extra_ref):
    ny = before_ref.shape[0]
    t, a, ground, left = (mat_ref[k] for k in range(4))
    f0 = -side_ref[2] * before_ref[...]
    extra = f0 / left
    j = side_ref[0] + f0 - (a + t) * extra
    q = side_ref[1] + t * extra + side_ref[3] * after_ref[0:ny, :]
    extra_ref[...] = extra
    store_values(buf_ref, [t, ground + after_ref[ny:, :], j, q])


def solve_kernel(n, m, halves, count, in_ref, out_ref):
    stride = m * count * halves

    def get(k):
        return jnp.concatenate(
            [
                in_ref[pl.ds((l * count + k) * halves + h, n, stride=stride), :]
                for l in range(m)
                for h in range(halves)
            ],
            axis=1,
        )

    t, g, j, q, *a = (get(k) for k in range(count))
    row = lax.broadcasted_iota(jnp.int32, t.shape, 0)
    first = row == 0
    last = row == n - 1

    def after(v, d=1):
        return pltpu.roll(v, n - d, 0)

    def before(v, d=1):
        return pltpu.roll(v, d, 0)

    g = g + jnp.where(first, t, 0.0)
    if a:
        g = g + jnp.where(last, 0.0, after(a[0]))
    low = jnp.where(first, 0.0, t)
    high = jnp.where(last, 0.0, after(t))
    r = q + jnp.where(last, 0.0, after(j))
    d = 1
    while d < n:
        inv = 1.0 / (g + low + high)
        gi = g * inv
        ri = r * inv
        g, r, low, high = (
            g + low * before(gi, d) + high * after(gi, d),
            r + low * before(ri, d) + high * after(ri, d),
            low * before(low * inv, d),
            high * after(high * inv, d),
        )
        d *= 2
    u = r / g
    u_prev = jnp.where(first, 0.0, before(u))
    for l in range(m):
        for k, value in enumerate((u_prev, u)):
            for h in range(halves):
                at = (l * halves + h) * LANES
                out_ref[pl.ds((l * 2 + k) * halves + h, n, stride=m * 2 * halves), :] = value[
                    :, at : at + LANES
                ]


def backward(n, u_prev, u_own, gam_ref, tau_ref, phi_ref, emit):
    u = u_own
    emit(n - 1, u)
    for i in range(n - 2, -1, -1):
        u = (phi_ref[i] + tau_ref[i] * u_prev) + gam_ref[i] * u
        emit(i, u)


def middle_kernel(
    shape, ends_ref, extra_ref, phi_x_ref, gam_x_ref, tau_x_ref, c_ref,
    phi_ref, gam_ref, tau_ref, buf_ref, half_ref,
):
    nx, ny, nz = shape
    u_prev, u_own = load_values(ends_ref, ny, 2, nz // LANES)
    backward(nx, u_prev + extra_ref[...], u_own, gam_x_ref, tau_x_ref, phi_x_ref,
             lambda i, u: store_plane(half_ref, shape, i, u))
    t = STEP * load_y_whole(c_ref, shape, 0)
    a = jnp.zeros_like(t)
    ground = jnp.ones_like(t)
    q = j = 0.0
    for y in range(ny - 1):
        c = STEP * load_y_whole(c_ref, shape, y + 1)
        h = load_y(half_ref, shape, y) + q
        inv = 1.0 / (t + ground + c)
        gam = c * inv
        tau = t * inv
        phi_ref[y] = inv * h
        gam_ref[y] = gam
        tau_ref[y] = tau
        q = gam * h
        j = j + tau * h
        a = a + tau * ground
        ground = 1.0 + gam * ground
        t = t * gam
    q = q + load_y(half_ref, shape, ny - 1)
    store_values(buf_ref, [t, ground, j, q, a])


def backward_y_kernel(shape, ends_ref, phi_ref, gam_ref, tau_ref, out_hbm, out_ref, sem):
    nx, ny, nz = shape
    u_prev, u_own = load_values(ends_ref, nx, 2, nz // LANES)
    copies = []

    def emit(y, u):
        store_y(out_ref, shape, y, u)
        if y % SUB == 0:
            copies.append(y_block_out(out_ref, out_hbm, y // SUB, sem))
            copies[-1].start()

    backward(ny, u_prev, u_own, gam_ref, tau_ref, phi_ref, emit)
    for copy in copies:
        copy.wait()


IN_VMEM = pl.BlockSpec(memory_space=pltpu.VMEM)
IN_HBM = pl.BlockSpec(memory_space=pltpu.HBM)


def call(kernel, args, outs, name, scratch=(), hbm_outs=(), bytes_accessed=1 << 20):
    return pl.pallas_call(
        kernel,
        out_shape=[jax.ShapeDtypeStruct(s, f32) for s in outs],
        in_specs=[IN_VMEM] * len(args),
        out_specs=[IN_HBM if k in hbm_outs else IN_VMEM for k in range(len(outs))],
        scratch_shapes=list(scratch),
        compiler_params=pltpu.CompilerParams(vmem_limit_bytes=16 * MIB),
        cost_estimate=pl.CostEstimate(flops=1 << 20, bytes_accessed=bytes_accessed, transcendentals=0),
        name=name,
    )(*args)


def shift(value, axis, up):
    count = lax.axis_size(axis)
    pairs = [(i, i + 1) for i in range(count - 1)]
    return lax.ppermute(value, axis, pairs if up else [(j, i) for i, j in pairs])


def exchange(buf, axis):
    n = lax.axis_size(axis)
    rows, lanes = buf.shape
    got = lax.all_to_all(buf.reshape(n, 1, rows * lanes // n), axis, 0, 0, tiled=True)
    return got.reshape(rows, lanes)


def interfaces(buf, axis, lines, halves, count):
    n = lax.axis_size(axis)
    m = lines // n
    every = exchange(buf, axis)
    kernel = functools.partial(solve_kernel, n, m, halves, count)
    (ends,) = call(kernel, [every], [(n * m * 2 * halves, LANES)], "solve_" + axis)
    return exchange(ends, axis)


def shards(field, cond_x, cond_y, cross_weight):
    shape = nx, ny, nz = field.shape
    halves = nz // LANES
    x_plane = (ny, nz)
    y_plane = (nx, nz)
    blocks = pltpu.SemaphoreType.DMA((ny // SUB,))
    below = shift(field[:, ny - 1, :], "gy", True)
    above = shift(field[:, 0, :], "gy", False)
    inv_x, gam_x, tau_x, mat_x = call(
        matrix_x_kernel, [cond_x], [(nx - 1, *x_plane)] * 3 + [(4, *x_plane)], "matrix_x",
        bytes_accessed=4 << 20,
    )
    up, down = call(
        rim_kernel, [field, below, above, mat_x], [x_plane, (2 * ny, nz)], "rim"
    )
    before = shift(up, "gx", True)
    after = shift(down, "gx", False)
    phi_x, side = call(
        forward_x_kernel, [field, cross_weight, below, above, inv_x, gam_x, tau_x],
        [(nx - 1, *x_plane), (4, *x_plane)], "forward_x",
        bytes_accessed=4 << 20,
    )
    buf_x, extra = call(
        finish_x_kernel, [before, after, mat_x, side], [(ny * 4 * halves, LANES), x_plane], "finish_x"
    )
    ends_x = interfaces(buf_x, "gx", ny, halves, 4)
    phi_y, gam_y, tau_y, buf_y = call(
        functools.partial(middle_kernel, shape),
        [ends_x, extra, phi_x, gam_x, tau_x, tile_rows(cond_y)],
        [(ny - 1, *y_plane)] * 3 + [(nx * 5 * halves, LANES)], "middle",
        scratch=(y_scratch(shape),),
    )
    ends_y = interfaces(buf_y, "gy", nx, halves, 5)
    (out,) = call(
        functools.partial(backward_y_kernel, shape), [ends_y, phi_y, gam_y, tau_y],
        [(nx, ny // SUB, SUB * halves, LANES)], "backward_y",
        scratch=(y_scratch(shape), blocks), hbm_outs=(0,),
    )
    return from_y_blocks(out, shape)


def solution(mesh):
    spec = P("gx", "gy", None)
    return jax.shard_map(
        shards, mesh=mesh, in_specs=(spec,) * 4, out_specs=spec, check_vma=False
    )
```

time: 108 us -> 98.4 us (0.911)
  blocking collectives: 62.3 us -> 77.7 us
  waiting for transfers between devices: 12 us -> 0.3 us
  local copies, waits for them, and re-layouts: 12.2 us -> 2.41 us
  starting transfers between devices: 15.5 us -> 13.5 us
  Pallas kernels: 5.49 us -> 3.98 us
    all_to_all x3 -> x4, blocking collectives: 62.3 us -> 77.7 us  [exchange(): lax.all_to_all(buf.reshape(n, 1, rows * lanes // n), axis, 0, 0, tiled=True)]
    all_to_all x1 -> x0, waiting for transfers between devices: 10.4 us -> none  [exchange(): lax.all_to_all(buf.reshape(n, 1, rows * lanes // n), axis, 0, 0, tiled=True)]
    unnamed x24 -> x10, local copies, waits for them, and re-layouts: 10.3 us -> 1.24 us
    all_to_all x1 -> x0, starting transfers between devices: 3.84 us -> none  [exchange(): lax.all_to_all(buf.reshape(n, 1, rows * lanes // n), axis, 0, 0, tiled=True)]
    ppermute x4, starting transfers between devices: 11.7 us -> 13.5 us  [shift(): lax.ppermute(value, axis, pairs if up else [(j, i) for i, j in pairs])]
    pallas_call x8, Pallas kernels: 5.49 us -> 3.98 us  [call(): pl.pallas_call(kernel, out_shape=[jax.ShapeDtypeStruct(s, f32) for s in o...]
    ppermute x4, waiting for transfers between devices: 1.58 us -> 0.3 us  [shift(): lax.ppermute(value, axis, pairs if up else [(j, i) for i, j in pairs])]
  transfers between devices with their start and end apart: 5 -> 4, of which waited for: 3 -> 1; matrix products, arithmetic and copies ran while one was open for 1% -> 0% of each run, Pallas kernels for 1% -> 1%
where the time goes in v1:
time: 98.4 us; the launch traced here: 98 us
  blocking collectives  77.7 us (79%)
  starting transfers between devices  13.5 us (14%)
  Pallas kernels  3.98 us (4%)
  local copies, waits for them, and re-layouts  2.41 us (2%)
    all_to_all x4, blocking collectives, exchange(): lax.all_to_all(buf.reshape(n, 1, rows * lanes // n), axis, 0, 0, tiled=True)  77.7 us
    ppermute x4, starting transfers between devices, shift(): lax.ppermute(value, axis, pairs if up else [(j, i) for i, j in pairs])  13.5 us
    pallas_call x8, Pallas kernels, call(): pl.pallas_call(kernel, out_shape=[jax.ShapeDtypeStruct(s, f32) for s in o...  3.98 us
  transfers between devices with their start and end apart: 4, of which 1 were waited for; matrix products, arithmetic and copies ran while one was open for 0% of the time, Pallas kernels for 1%

profile of v1, /device:TPU:2, one launch (start us, length us, event | category | flops | bytes accessed | tf_op | source)
XLA Modules:
  0.0 98.0 jit_solution(14216880064419554595)
XLA Ops:
  0.0 0.0 copy-start
  0.0 1.2 %fusion = (f32[32,1,256]{2,1,0:T(1,128)S(1)}, f32[32,1,256]{2,1,0:T(1,128)S(1)}) fusion(f32[32,32,256]{2,1,0:T(8,128)} %field_ref.3), kind=kLoop, calls=%fused_computation.2 | loop fusion | bytes 131072 | tf_op jit(solution)/shard_map/slice | solution.py:320
  1.2 3.4 %collective-permute-start = (f32[32,256]{1,0:T(8,128)S(1)}, f32[32,256]{1,0:T(8,128)S(1)}, u32[]{:S(2)}, u32[]{:S(2)}) collective-permute-start(f32[32,256]{1,0:T(8,128)S(1)} %bitcast.33), channel_id=1, source_target_pairs={{0,1},{1,2},{2,3},{3,4},{4,5},{5,6},{6,7},{7,8},{8,9},{9,10},{10,1... | collective-permute-start | bytes 98312 | tf_op jit(solution)/shard_map/ppermute | solution.py:294
  4.6 0.0 copy-start.1
  4.6 5.8 %collective-permute-start.1 = (f32[32,256]{1,0:T(8,128)S(1)}, f32[32,256]{1,0:T(8,128)S(1)}, u32[]{:S(2)}, u32[]{:S(2)}) collective-permute-start(f32[32,256]{1,0:T(8,128)S(1)} %bitcast.34), channel_id=1, source_target_pairs={{1,0},{2,1},{3,2},{4,3},{5,4},{6,5},{7,6},{8,7},{9,8},{10,9},{11,1... | collective-permute-start | bytes 98312 | tf_op jit(solution)/shard_map/ppermute | solution.py:294
  10.4 0.0 copy-start.2
  10.4 1.2 %copy-done.2 = f32[32,32,256]{2,1,0:T(8,128)S(1)} copy-done((f32[32,32,256]{2,1,0:T(8,128)S(1)}, f32[32,32,256]{2,1,0:T(8,128)}, u32[]{:S(2)}) %copy-start.2) | copy-done | bytes 1048600
  11.7 0.5 matrix_x.1
  12.1 0.0 collective-permute-done.below_ref
  12.1 0.0 collective-permute-done.1.above_ref
  12.2 0.0 copy-done
  12.2 1.3 %collective-permute-start.3 = (f32[64,256]{1,0:T(8,128)S(1)}, f32[64,256]{1,0:T(8,128)S(1)}, u32[]{:S(2)}, u32[]{:S(2)}) collective-permute-start(f32[64,256]{1,0:T(8,128)S(1)} %get-tuple-element.21), channel_id=1, source_target_pairs={{16,0},{32,16},{48,32},{64,48},{80,64},{96,80},{112,96},{128,112},... | collective-permute-start | bytes 196616 | tf_op jit(solution)/shard_map/ppermute | solution.py:294
  13.5 3.0 %collective-permute-start.2 = (f32[32,256]{1,0:T(8,128)S(1)}, f32[32,256]{1,0:T(8,128)S(1)}, u32[]{:S(2)}, u32[]{:S(2)}) collective-permute-start(f32[32,256]{1,0:T(8,128)S(1)} %get-tuple-element.20), channel_id=1, source_target_pairs={{0,16},{16,32},{32,48},{48,64},{64,80},{80,96},{96,112},{112,128},... | collective-permute-start | bytes 98312 | tf_op jit(solution)/shard_map/ppermute | solution.py:294
  16.5 0.0 copy-done.1
  16.5 0.0 copy-start.3
  16.6 0.5 forward_x.1
  17.1 0.3 collective-permute-done.2.before_ref
  17.4 0.0 collective-permute-done.3.after_ref
  17.4 34.0 %all_to_all.20 = f32[32,1,1024]{2,1,0:T(1,128)S(1)} all-to-all(f32[32,1,1024]{2,1,0:T(1,128)S(1)} %bitcast.32), channel_id=1, replica_groups=mesh['gx'=32,'gy'=16] {'gx'}, dimensions={0} | all-to-all | bytes 262144 | tf_op jit(solution)/shard_map/all_to_all | solution.py:300
  51.5 0.2 solve_gx.1
  51.6 17.3 %all_to_all.21 = f32[32,1,512]{2,1,0:T(1,128)S(1)} all-to-all(f32[32,1,512]{2,1,0:T(1,128)S(1)} %bitcast.29), channel_id=1, replica_groups=mesh['gx'=32,'gy'=16] {'gx'}, dimensions={0} | all-to-all | bytes 131072 | tf_op jit(solution)/shard_map/all_to_all | solution.py:300
  68.9 0.0 copy-done.3
  68.9 1.4 %middle.1 = (f32[31,32,256]{2,1,0:T(8,128)S(1)}, f32[31,32,256]{2,1,0:T(8,128)S(1)}, f32[31,32,256]{2,1,0:T(8,128)S(1)}, f32[320,128]{1,0:T(8,128)S(1)}) custom-call(f32[128,128]{1,0:T(8,128)S(1)} %bitcast.27, f32[32,256]{1,0:T(8,128)S(1)} %get-tuple-element.27.extra_ref, f32[31,32,256]{2,1,0:T(8,128)S(1)} %get-tuple-element.28.phi_x_ref, ...), custom_call_target="tpu_custom_call" | custom-call | flops 1048576 | bytes 1048576 | tf_op jit(solution)/shard_map/middle/pallas_call | solution.py:279
  70.3 15.6 %all_to_all.22 = f32[16,1,2560]{2,1,0:T(1,128)S(1)} all-to-all(f32[16,1,2560]{2,1,0:T(1,128)S(1)} %bitcast.31), channel_id=1, replica_groups=mesh['gx'=32,'gy'=16] {'gy'}, dimensions={0} | all-to-all | bytes 327680 | tf_op jit(solution)/shard_map/all_to_all | solution.py:300
  85.9 0.1 solve_gy.1
  86.1 10.7 %all_to_all.23 = f32[16,1,1024]{2,1,0:T(1,128)S(1)} all-to-all(f32[16,1,1024]{2,1,0:T(1,128)S(1)} %bitcast.30), channel_id=1, replica_groups=mesh['gx'=32,'gy'=16] {'gy'}, dimensions={0} | all-to-all | bytes 131072 | tf_op jit(solution)/shard_map/all_to_all | solution.py:300
  96.8 1.2 %backward_y.1 = f32[32,4,16,128]{3,2,1,0:T(8,128)} custom-call(f32[128,128]{1,0:T(8,128)S(1)} %bitcast.28, f32[31,32,256]{2,1,0:T(8,128)S(1)} %get-tuple-element.30.phi_ref, f32[31,32,256]{2,1,0:T(8,128)S(1)} %get-tuple-element.31.gam_ref, f32[31,32,256]{2,1,0:T(8,128)S(1)} %get-tuple-element.32.tau_ref), custom_call_target="tpu_custom_call" | custom-call | flops 1048576 | bytes 1048576 | tf_op jit(solution)/shard_map/backward_y/pallas_call | solution.py:279
  (4 shorter events, 0.1 us)
Async XLA Ops:
  0.0 12.2 %copy-start = (f32[32,32,256]{2,1,0:T(8,128)S(1)}, f32[32,32,256]{2,1,0:T(8,128)}, u32[]{:S(2)}) copy-start(f32[32,32,256]{2,1,0:T(8,128)} %field_ref.3) | copy-start | bytes 3145732
  1.2 11.0 %collective-permute-start = (f32[32,256]{1,0:T(8,128)S(1)}, f32[32,256]{1,0:T(8,128)S(1)}, u32[]{:S(2)}, u32[]{:S(2)}) collective-permute-start(f32[32,256]{1,0:T(8,128)S(1)} %bitcast.33), channel_id=1, source_target_pairs={{0,1},{1,2},{2,3},{3,4},{4,5},{5,6},{6,7},{7,8},{8,9},{9,10},{10,1... | collective-permute-start | bytes 98312 | tf_op jit(solution)/shard_map/ppermute | solution.py:294
  4.6 11.9 %copy-start.1 = (f32[32,32,256]{2,1,0:T(8,128)S(1)}, f32[32,32,256]{2,1,0:T(8,128)}, u32[]{:S(2)}) copy-start(f32[32,32,256]{2,1,0:T(8,128)} %weight_ref.1) | copy-start | bytes 3145732
  4.6 7.5 %collective-permute-start.1 = (f32[32,256]{1,0:T(8,128)S(1)}, f32[32,256]{1,0:T(8,128)S(1)}, u32[]{:S(2)}, u32[]{:S(2)}) collective-permute-start(f32[32,256]{1,0:T(8,128)S(1)} %bitcast.34), channel_id=1, source_target_pairs={{1,0},{2,1},{3,2},{4,3},{5,4},{6,5},{7,6},{8,7},{9,8},{10,9},{11,1... | collective-permute-start | bytes 98312 | tf_op jit(solution)/shard_map/ppermute | solution.py:294
  10.4 1.2 %copy-start.2 = (f32[32,32,256]{2,1,0:T(8,128)S(1)}, f32[32,32,256]{2,1,0:T(8,128)}, u32[]{:S(2)}) copy-start(f32[32,32,256]{2,1,0:T(8,128)} %c_ref.1) | copy-start | bytes 3145732
  12.2 5.2 %collective-permute-start.3 = (f32[64,256]{1,0:T(8,128)S(1)}, f32[64,256]{1,0:T(8,128)S(1)}, u32[]{:S(2)}, u32[]{:S(2)}) collective-permute-start(f32[64,256]{1,0:T(8,128)S(1)} %get-tuple-element.21), channel_id=1, source_target_pairs={{16,0},{32,16},{48,32},{64,48},{80,64},{96,80},{112,96},{128,112},... | collective-permute-start | bytes 196616 | tf_op jit(solution)/shard_map/ppermute | solution.py:294
  13.5 3.9 %collective-permute-start.2 = (f32[32,256]{1,0:T(8,128)S(1)}, f32[32,256]{1,0:T(8,128)S(1)}, u32[]{:S(2)}, u32[]{:S(2)}) collective-permute-start(f32[32,256]{1,0:T(8,128)S(1)} %get-tuple-element.20), channel_id=1, source_target_pairs={{0,16},{16,32},{32,48},{48,64},{64,80},{80,96},{96,112},{112,128},... | collective-permute-start | bytes 98312 | tf_op jit(solution)/shard_map/ppermute | solution.py:294
  16.5 52.4 %copy-start.3 = (f32[32,32,256]{2,1,0:T(8,128)S(1)}, f32[32,32,256]{2,1,0:T(8,128)}, u32[]{:S(2)}) copy-start(f32[32,32,256]{2,1,0:T(8,128)} %param.6) | copy-start | bytes 3145732

commit v2 on v1

--- a/solution.py
+++ b/solution.py
@@ -11,6 +11,7 @@
 LANES = 128
 SUB = 8
 MIB = 1 << 20
+MOST_VMEM = 66322432
 f32 = jnp.float32
 
 
@@ -90,14 +91,75 @@
     ]
 
 
-def matrix_x_kernel(c_ref, inv_ref, gam_ref, tau_ref, mat_ref):
+def pack_kernel(field_hbm, weight_hbm, c_hbm, rows_ref, field_ref, weight_ref, c_ref, sem):
+    tile = pl.ds(field_hbm.shape[1] - SUB, SUB)
+    copies = [
+        pltpu.make_async_copy(hbm.at[:, tile, :], ref, sem.at[k])
+        for k, (hbm, ref) in enumerate(
+            ((field_hbm, field_ref), (weight_hbm, weight_ref), (c_hbm, c_ref))
+        )
+    ]
+    for copy in copies:
+        copy.start()
+    for copy in copies:
+        copy.wait()
+    rows_ref[0] = field_ref[:, SUB - 1, :]
+    rows_ref[1] = field_ref[:, SUB - 2, :]
+    rows_ref[2] = weight_ref[:, SUB - 1, :]
+    rows_ref[3] = c_ref[:, SUB - 1, :]
+
+
+def stage_kernel(field_ref, weight_ref, c_ref, token_ref):
+    token_ref[...] = field_ref[0, 0:SUB, 0:LANES] + weight_ref[0, 0:SUB, 0:LANES] + c_ref[0, 0:SUB, 0:LANES]
+
+
+def not_first(axis):
+    return jnp.where(lax.axis_index(axis) == 0, 0.0, 1.0).astype(f32)
+
+
+class Rows:
+    def __init__(self, shape, rows_ref, inside):
+        self.n = shape[0]
+        self.row = lax.broadcasted_iota(jnp.int32, shape, 0)
+        self.rows_ref = rows_ref
+        self.inside = inside
+
+    def put(self, place, row, plane):
+        return jnp.where(self.row == place, row, plane)
+
+    def got(self, k, i):
+        return self.rows_ref[k, i : i + 1, :]
+
+    def plane(self, ref, k, i):
+        return self.put(self.n - 1, self.got(k, i), ref[i])
+
+    def difference(self, ref, i):
+        n = self.n
+        plane = ref[i]
+        up = pltpu.roll(plane, n - 1, 0)
+        up = self.put(n - 1, up * self.inside, up)
+        down = pltpu.roll(plane, 1, 0)
+        down = self.put(0, self.got(0, i) * self.inside, down)
+        return up - self.put(n - 1, self.got(1, i), down)
+
+
+def matrix_x_kernel(
+    field_ref, weight_ref, c_ref, rows_ref, token_ref,
+    inv_ref, gam_ref, tau_ref, mat_ref, up_ref,
+):
     n = c_ref.shape[0]
-    left = STEP * c_ref[0]
+    rows = Rows(c_ref.shape[1:], rows_ref, not_first("gy"))
+    up_ref[0] = rows.difference(field_ref, n - 1)
+    weight = rows.plane(weight_ref, 2, n - 1) * 0.25
+    before = rows.difference(field_ref, n - 2)
+    up_ref[1] = rows.plane(field_ref, 0, n - 1) - weight * before
+    up_ref[2] = weight
+    left = STEP * rows.plane(c_ref, 3, 0)
     t = left
     a = jnp.zeros_like(t)
     ground = jnp.ones_like(t)
     for i in range(n - 1):
-        c = STEP * c_ref[i + 1]
+        c = STEP * rows.plane(c_ref, 3, i + 1)
         inv = 1.0 / (t + ground + c)
         gam = c * inv
         tau = t * inv
@@ -107,61 +169,42 @@
         a = a + tau * ground
         ground = 1.0 + gam * ground
         t = t * gam
-    for k, value in enumerate((t, a, ground, left)):
+    up_ref[3] = ground + t * (1.0 - not_first("gx"))
+    for k, value in enumerate((t, a, left)):
         mat_ref[k] = value
 
 
-def y_difference(plane, below, above):
-    n = plane.shape[0]
-    row = lax.broadcasted_iota(jnp.int32, plane.shape, 0)
-    up = jnp.where(row == n - 1, above, pltpu.roll(plane, n - 1, 0))
-    down = jnp.where(row == 0, below, pltpu.roll(plane, 1, 0))
-    return up - down
-
-
-def rim_kernel(field_ref, below_ref, above_ref, mat_ref, up_ref, down_ref):
-    n = field_ref.shape[0]
-    ny = field_ref.shape[1]
-    up_ref[...] = y_difference(field_ref[n - 1], below_ref[n - 1 : n, :], above_ref[n - 1 : n, :])
-    down_ref[0:ny, :] = y_difference(field_ref[0], below_ref[0:1, :], above_ref[0:1, :])
-    down_ref[ny:, :] = mat_ref[1]
-
-
 def forward_x_kernel(
-    field_ref, weight_ref, below_ref, above_ref, inv_ref, gam_ref, tau_ref, phi_ref, side_ref,
+    field_ref, weight_ref, rows_ref, inv_ref, gam_ref, tau_ref, phi_ref, side_ref,
 ):
     n = field_ref.shape[0]
-    diffs = {}
-
-    def diff(i):
-        if not 0 <= i < n:
-            return 0.0
-        if i not in diffs:
-            diffs[i] = y_difference(field_ref[i], below_ref[i : i + 1, :], above_ref[i : i + 1, :])
-        return diffs[i]
-
+    rows = Rows(field_ref.shape[1:], rows_ref, not_first("gy"))
+    diffs = {-1: 0.0, 0: rows.difference(field_ref, 0)}
+    side_ref[3] = diffs[0]
     q = j = 0.0
-    for i in range(n):
-        mixed = diff(i + 1) - diff(i - 1)
-        diffs.pop(i - 1, None)
-        h = field_ref[i] + weight_ref[i] * mixed * 0.25 + q
-        if i < n - 1:
-            phi_ref[i] = inv_ref[i] * h
-            q = gam_ref[i] * h
-            j = j + tau_ref[i] * h
-    for k, value in enumerate((j, h, weight_ref[0] * 0.25, weight_ref[n - 1] * 0.25)):
-        side_ref[k] = value
-
-
-def finish_x_kernel(before_ref, after_ref, mat_ref, side_ref, buf_ref, extra_ref):
-    ny = before_ref.shape[0]
-    t, a, ground, left = (mat_ref[k] for k in range(4))
-    f0 = -side_ref[2] * before_ref[...]
+    for i in range(n - 1):
+        diffs[i + 1] = rows.difference(field_ref, i + 1)
+        weight = rows.plane(weight_ref, 2, i) * 0.25
+        if i == 0:
+            side_ref[2] = weight
+        h = rows.plane(field_ref, 0, i) + weight * (diffs[i + 1] - diffs.pop(i - 1)) + q
+        phi_ref[i] = inv_ref[i] * h
+        q = gam_ref[i] * h
+        j = j + tau_ref[i] * h
+    side_ref[0] = j
+    side_ref[1] = q
+
+
+def finish_x_kernel(got_ref, mat_ref, side_ref, buf_ref, extra_ref):
+    inside = not_first("gx")
+    t, a, left = (mat_ref[k] for k in range(3))
+    f0 = side_ref[2] * got_ref[0] * -inside
     extra = f0 / left
-    j = side_ref[0] + f0 - (a + t) * extra
-    q = side_ref[1] + t * extra + side_ref[3] * after_ref[0:ny, :]
+    source = got_ref[1] + got_ref[2] * side_ref[3] * inside
+    j = (side_ref[0] + f0 - (a + t) * extra) * inside + source
+    q = side_ref[1] + t * extra
     extra_ref[...] = extra
-    store_values(buf_ref, [t, ground + after_ref[ny:, :], j, q])
+    store_values(buf_ref, [t * inside, got_ref[3] + a * inside, j, q])
 
 
 def solve_kernel(n, m, halves, count, in_ref, out_ref):
@@ -177,23 +220,18 @@
             axis=1,
         )
 
-    t, g, j, q, *a = (get(k) for k in range(count))
-    row = lax.broadcasted_iota(jnp.int32, t.shape, 0)
-    first = row == 0
-    last = row == n - 1
-
     def after(v, d=1):
         return pltpu.roll(v, n - d, 0)
 
     def before(v, d=1):
         return pltpu.roll(v, d, 0)
 
-    g = g + jnp.where(first, t, 0.0)
-    if a:
-        g = g + jnp.where(last, 0.0, after(a[0]))
-    low = jnp.where(first, 0.0, t)
-    high = jnp.where(last, 0.0, after(t))
-    r = q + jnp.where(last, 0.0, after(j))
+    low, g, j, q, *ground = (get(k) for k in range(count))
+    g = after(g)
+    if ground:
+        g = g + ground[0]
+    high = after(low)
+    r = q + after(j)
     d = 1
     while d < n:
         inv = 1.0 / (g + low + high)
@@ -207,7 +245,7 @@
         )
         d *= 2
     u = r / g
-    u_prev = jnp.where(first, 0.0, before(u))
+    u_prev = before(u)
     for l in range(m):
         for k, value in enumerate((u_prev, u)):
             for h in range(halves):
@@ -231,7 +269,7 @@
 ):
     nx, ny, nz = shape
     u_prev, u_own = load_values(ends_ref, ny, 2, nz // LANES)
-    backward(nx, u_prev + extra_ref[...], u_own, gam_x_ref, tau_x_ref, phi_x_ref,
+    backward(nx, u_prev * not_first("gx") + extra_ref[...], u_own, gam_x_ref, tau_x_ref, phi_x_ref,
              lambda i, u: store_plane(half_ref, shape, i, u))
     t = STEP * load_y_whole(c_ref, shape, 0)
     a = jnp.zeros_like(t)
@@ -251,8 +289,9 @@
         a = a + tau * ground
         ground = 1.0 + gam * ground
         t = t * gam
-    q = q + load_y(half_ref, shape, ny - 1)
-    store_values(buf_ref, [t, ground, j, q, a])
+    inside = not_first("gy")
+    j = j * inside + load_y(half_ref, shape, ny - 1)
+    store_values(buf_ref, [t * inside, a * inside, j, q, ground + t * (1.0 - inside)])
 
 
 def backward_y_kernel(shape, ends_ref, phi_ref, gam_ref, tau_ref, out_hbm, out_ref, sem):
@@ -266,32 +305,32 @@
             copies.append(y_block_out(out_ref, out_hbm, y // SUB, sem))
             copies[-1].start()
 
-    backward(ny, u_prev, u_own, gam_ref, tau_ref, phi_ref, emit)
+    backward(ny, u_prev * not_first("gy"), u_own, gam_ref, tau_ref, phi_ref, emit)
     for copy in copies:
         copy.wait()
 
 
 IN_VMEM = pl.BlockSpec(memory_space=pltpu.VMEM)
-IN_HBM = pl.BlockSpec(memory_space=pltpu.HBM)
-
-
-def call(kernel, args, outs, name, scratch=(), hbm_outs=(), bytes_accessed=1 << 20):
+IN_PLACE = pl.BlockSpec(memory_space=pl.ANY)
+
+
+def call(kernel, args, outs, name, scratch=(), hbm_args=(), hbm_outs=(), bytes_accessed=1 << 20,
+         limit=16 * MIB):
     return pl.pallas_call(
         kernel,
         out_shape=[jax.ShapeDtypeStruct(s, f32) for s in outs],
-        in_specs=[IN_VMEM] * len(args),
-        out_specs=[IN_HBM if k in hbm_outs else IN_VMEM for k in range(len(outs))],
+        in_specs=[IN_PLACE if k in hbm_args else IN_VMEM for k in range(len(args))],
+        out_specs=[IN_PLACE if k in hbm_outs else IN_VMEM for k in range(len(outs))],
         scratch_shapes=list(scratch),
-        compiler_params=pltpu.CompilerParams(vmem_limit_bytes=16 * MIB),
+        compiler_params=pltpu.CompilerParams(vmem_limit_bytes=limit),
         cost_estimate=pl.CostEstimate(flops=1 << 20, bytes_accessed=bytes_accessed, transcendentals=0),
         name=name,
     )(*args)
 
 
-def shift(value, axis, up):
-    count = lax.axis_size(axis)
-    pairs = [(i, i + 1) for i in range(count - 1)]
-    return lax.ppermute(value, axis, pairs if up else [(j, i) for i, j in pairs])
+def from_before(value, axis):
+    n = lax.axis_size(axis)
+    return lax.ppermute(value, axis, [(i, (i + 1) % n) for i in range(n)])
 
 
 def exchange(buf, axis):
@@ -316,24 +355,25 @@
     x_plane = (ny, nz)
     y_plane = (nx, nz)
     blocks = pltpu.SemaphoreType.DMA((ny // SUB,))
-    below = shift(field[:, ny - 1, :], "gy", True)
-    above = shift(field[:, 0, :], "gy", False)
-    inv_x, gam_x, tau_x, mat_x = call(
-        matrix_x_kernel, [cond_x], [(nx - 1, *x_plane)] * 3 + [(4, *x_plane)], "matrix_x",
-        bytes_accessed=4 << 20,
-    )
-    up, down = call(
-        rim_kernel, [field, below, above, mat_x], [x_plane, (2 * ny, nz)], "rim"
-    )
-    before = shift(up, "gx", True)
-    after = shift(down, "gx", False)
+    tile = pltpu.VMEM((nx, SUB, nz), f32)
+    (rows,) = call(
+        pack_kernel, [field, cross_weight, cond_x], [(4, *y_plane)], "pack",
+        scratch=(tile, tile, tile, pltpu.SemaphoreType.DMA((3,))), hbm_args=(0, 1, 2),
+        limit=MOST_VMEM,
+    )
+    rows = from_before(rows, "gy")
+    (token,) = call(stage_kernel, [field, cross_weight, cond_x], [(SUB, LANES)], "stage")
+    inv_x, gam_x, tau_x, mat_x, up = call(
+        matrix_x_kernel, [field, cross_weight, cond_x, rows, token],
+        [(nx - 1, *x_plane)] * 3 + [(3, *x_plane), (4, *x_plane)], "matrix_x",
+    )
+    got = from_before(up, "gx")
     phi_x, side = call(
-        forward_x_kernel, [field, cross_weight, below, above, inv_x, gam_x, tau_x],
-        [(nx - 1, *x_plane), (4, *x_plane)], "forward_x",
-        bytes_accessed=4 << 20,
+        forward_x_kernel, [field, cross_weight, rows, inv_x, gam_x, tau_x],
+        [(nx - 1, *x_plane), (4, *x_plane)], "forward_x", bytes_accessed=4 << 20,
     )
     buf_x, extra = call(
-        finish_x_kernel, [before, after, mat_x, side], [(ny * 4 * halves, LANES), x_plane], "finish_x"
+        finish_x_kernel, [got, mat_x, side], [(ny * 4 * halves, LANES), x_plane], "finish_x"
     )
     ends_x = interfaces(buf_x, "gx", ny, halves, 4)
     phi_y, gam_y, tau_y, buf_y = call(

time: 98.4 us -> 93.2 us (0.947)
  waiting for transfers between devices: 0.3 us -> 10.7 us
  starting transfers between devices: 13.5 us -> 3.42 us
  blocking collectives: 77.7 us -> 69.1 us
  Pallas kernels: 3.98 us -> 5.92 us
  local copies, waits for them, and re-layouts: 2.41 us -> 3.67 us
    ppermute x4 -> x2, waiting for transfers between devices: 0.3 us -> 10.7 us  [from_before(): return lax.ppermute(value, axis, [(i, (i + 1) % n) for i in range(n)])]
    ppermute x4 -> x2, starting transfers between devices: 13.5 us -> 3.42 us  [from_before(): return lax.ppermute(value, axis, [(i, (i + 1) % n) for i in range(n)])]
    all_to_all x4, blocking collectives: 77.7 us -> 69.1 us  [exchange(): lax.all_to_all(buf.reshape(n, 1, rows * lanes // n), axis, 0, 0, tiled=True)]
    unnamed x10 -> x8, local copies, waits for them, and re-layouts: 1.24 us -> 3.67 us
    pallas_call x8 -> x9, Pallas kernels: 3.98 us -> 5.92 us  [call(): pl.pallas_call(kernel, out_shape=[jax.ShapeDtypeStruct(s, f32) for s in o...]
    slice x1 -> x0, local copies, waits for them, and re-layouts: 1.17 us -> none  [shards(): above = shift(field[:, 0, :], 'gy', False)]
  transfers between devices with their start and end apart: 4 -> 2, of which waited for: 1 -> 2; matrix products, arithmetic and copies ran while one was open for 0% -> 0% of each run, Pallas kernels for 1% -> 1%
where the time goes in v2:
time: 93.2 us; the launch traced here: 92.8 us
  blocking collectives  69.1 us (74%)
  waiting for transfers between devices  10.7 us (11%)
  Pallas kernels  5.92 us (6%)
  local copies, waits for them, and re-layouts  3.67 us (4%)
  starting transfers between devices  3.42 us (4%)
    all_to_all x4, blocking collectives, exchange(): lax.all_to_all(buf.reshape(n, 1, rows * lanes // n), axis, 0, 0, tiled=True)  69.1 us
    ppermute x2, waiting for transfers between devices, from_before(): return lax.ppermute(value, axis, [(i, (i + 1) % n) for i in range(n)])  10.7 us
    pallas_call x9, Pallas kernels, call(): pl.pallas_call(kernel, out_shape=[jax.ShapeDtypeStruct(s, f32) for s in o...  5.92 us
    unnamed x8, local copies, waits for them, and re-layouts  3.67 us
    ppermute x2, starting transfers between devices, from_before(): return lax.ppermute(value, axis, [(i, (i + 1) % n) for i in range(n)])  3.42 us
  transfers between devices with their start and end apart: 2, of which 2 were waited for; matrix products, arithmetic and copies ran while one was open for 0% of the time, Pallas kernels for 1%

profile of v2, /device:TPU:2, one launch (start us, length us, event | category | flops | bytes accessed | tf_op | source)
XLA Modules:
  0.0 92.8 jit_solution(4429546212156855468)
XLA Ops:
  0.0 1.8 %pack.1 = f32[4,32,256]{2,1,0:T(8,128)} custom-call(f32[32,32,256]{2,1,0:T(8,128)} %field_ref.5, f32[32,32,256]{2,1,0:T(8,128)} %weight_ref.5, f32[32,32,256]{2,1,0:T(8,128)} %c_ref.3), custom_call_target="tpu_custom_call" | custom-call | flops 1048576 | bytes 1048576 | tf_op jit(solution)/shard_map/pack/pallas_call | solution.py:319
  1.8 3.4 %collective-permute-start = (f32[4,32,256]{2,1,0:T(8,128)}, f32[4,32,256]{2,1,0:T(8,128)S(1)}, u32[]{:S(2)}, u32[]{:S(2)}) collective-permute-start(f32[4,32,256]{2,1,0:T(8,128)} %pack.1), channel_id=1, source_target_pairs={{0,1},{1,2},{2,3},{3,4},{4,5},{5,6},{6,7},{7,8},{8,9},{9,10},{10,1... | collective-permute-start | bytes 393224 | tf_op jit(solution)/shard_map/ppermute | solution.py:333
  5.3 0.0 copy-start
  5.3 1.2 %copy-done = f32[32,32,256]{2,1,0:T(8,128)S(1)} copy-done((f32[32,32,256]{2,1,0:T(8,128)S(1)}, f32[32,32,256]{2,1,0:T(8,128)}, u32[]{:S(2)}) %copy-start) | copy-done | bytes 1048600
  6.5 0.0 copy-start.1
  6.5 1.2 %copy-done.1 = f32[32,32,256]{2,1,0:T(8,128)S(1)} copy-done((f32[32,32,256]{2,1,0:T(8,128)S(1)}, f32[32,32,256]{2,1,0:T(8,128)}, u32[]{:S(2)}) %copy-start.1) | copy-done | bytes 1048600
  7.7 0.0 copy-start.2
  7.7 1.2 %copy-done.2 = f32[32,32,256]{2,1,0:T(8,128)S(1)} copy-done((f32[32,32,256]{2,1,0:T(8,128)S(1)}, f32[32,32,256]{2,1,0:T(8,128)}, u32[]{:S(2)}) %copy-start.2) | copy-done | bytes 1048600
  8.9 3.8 %collective-permute-done.rows_ref = f32[4,32,256]{2,1,0:T(8,128)S(1)} collective-permute-done((f32[4,32,256]{2,1,0:T(8,128)}, f32[4,32,256]{2,1,0:T(8,128)S(1)}, u32[]{:S(2)}, u32[]{:S(2)}) %collective-permute-start) | collective-permute-done | bytes 131104 | tf_op jit(solution)/shard_map/ppermute | solution.py:333
  12.8 0.5 matrix_x.1
  13.3 0.0 collective-permute-start.1
  13.3 0.0 copy-start.3
  13.3 0.6 forward_x.1
  13.9 6.8 %collective-permute-done.1.got_ref = f32[4,32,256]{2,1,0:T(8,128)S(1)} collective-permute-done((f32[4,32,256]{2,1,0:T(8,128)S(1)}, f32[4,32,256]{2,1,0:T(8,128)S(1)}, u32[]{:S(2)}, u32[]{:S(2)}) %collective-permute-start.1) | collective-permute-done | bytes 131104 | tf_op jit(solution)/shard_map/ppermute | solution.py:333
  20.8 27.0 %all_to_all.20 = f32[32,1,1024]{2,1,0:T(1,128)S(1)} all-to-all(f32[32,1,1024]{2,1,0:T(1,128)S(1)} %bitcast.26), channel_id=1, replica_groups=mesh['gx'=32,'gy'=16] {'gx'}, dimensions={0} | all-to-all | bytes 262144 | tf_op jit(solution)/shard_map/all_to_all | solution.py:339
  47.8 0.2 solve_gx.1
  48.0 17.3 %all_to_all.21 = f32[32,1,512]{2,1,0:T(1,128)S(1)} all-to-all(f32[32,1,512]{2,1,0:T(1,128)S(1)} %bitcast.23), channel_id=1, replica_groups=mesh['gx'=32,'gy'=16] {'gx'}, dimensions={0} | all-to-all | bytes 131072 | tf_op jit(solution)/shard_map/all_to_all | solution.py:339
  65.3 0.0 copy-done.3
  65.3 1.4 %middle.1 = (f32[31,32,256]{2,1,0:T(8,128)S(1)}, f32[31,32,256]{2,1,0:T(8,128)S(1)}, f32[31,32,256]{2,1,0:T(8,128)S(1)}, f32[320,128]{1,0:T(8,128)S(1)}) custom-call(f32[128,128]{1,0:T(8,128)S(1)} %bitcast.21, f32[32,256]{1,0:T(8,128)S(1)} %get-tuple-element.25.extra_ref, f32[31,32,256]{2,1,0:T(8,128)S(1)} %get-tuple-element.26.phi_x_ref, ...), custom_call_target="tpu_custom_call" | custom-call | flops 1048576 | bytes 1048576 | tf_op jit(solution)/shard_map/middle/pallas_call | solution.py:319
  66.7 14.1 %all_to_all.22 = f32[16,1,2560]{2,1,0:T(1,128)S(1)} all-to-all(f32[16,1,2560]{2,1,0:T(1,128)S(1)} %bitcast.25), channel_id=1, replica_groups=mesh['gx'=32,'gy'=16] {'gy'}, dimensions={0} | all-to-all | bytes 327680 | tf_op jit(solution)/shard_map/all_to_all | solution.py:339
  80.7 0.1 solve_gy.1
  80.9 10.7 %all_to_all.23 = f32[16,1,1024]{2,1,0:T(1,128)S(1)} all-to-all(f32[16,1,1024]{2,1,0:T(1,128)S(1)} %bitcast.24), channel_id=1, replica_groups=mesh['gx'=32,'gy'=16] {'gy'}, dimensions={0} | all-to-all | bytes 131072 | tf_op jit(solution)/shard_map/all_to_all | solution.py:339
  91.6 1.2 %backward_y.1 = f32[32,4,16,128]{3,2,1,0:T(8,128)} custom-call(f32[128,128]{1,0:T(8,128)S(1)} %bitcast.22, f32[31,32,256]{2,1,0:T(8,128)S(1)} %get-tuple-element.28.phi_ref, f32[31,32,256]{2,1,0:T(8,128)S(1)} %get-tuple-element.29.gam_ref, f32[31,32,256]{2,1,0:T(8,128)S(1)} %get-tuple-element.30.tau_ref), custom_call_target="tpu_custom_call" | custom-call | flops 1048576 | bytes 1048576 | tf_op jit(solution)/shard_map/backward_y/pallas_call | solution.py:319
  (2 shorter events, 0.0 us)
Async XLA Ops:
  1.8 10.9 %collective-permute-start = (f32[4,32,256]{2,1,0:T(8,128)}, f32[4,32,256]{2,1,0:T(8,128)S(1)}, u32[]{:S(2)}, u32[]{:S(2)}) collective-permute-start(f32[4,32,256]{2,1,0:T(8,128)} %pack.1), channel_id=1, source_target_pairs={{0,1},{1,2},{2,3},{3,4},{4,5},{5,6},{6,7},{7,8},{8,9},{9,10},{10,1... | collective-permute-start | bytes 393224 | tf_op jit(solution)/shard_map/ppermute | solution.py:333
  5.3 1.2 %copy-start = (f32[32,32,256]{2,1,0:T(8,128)S(1)}, f32[32,32,256]{2,1,0:T(8,128)}, u32[]{:S(2)}) copy-start(f32[32,32,256]{2,1,0:T(8,128)} %field_ref.5) | copy-start | bytes 3145732
  6.5 1.2 %copy-start.1 = (f32[32,32,256]{2,1,0:T(8,128)S(1)}, f32[32,32,256]{2,1,0:T(8,128)}, u32[]{:S(2)}) copy-start(f32[32,32,256]{2,1,0:T(8,128)} %weight_ref.5) | copy-start | bytes 3145732
  7.7 1.2 %copy-start.2 = (f32[32,32,256]{2,1,0:T(8,128)S(1)}, f32[32,32,256]{2,1,0:T(8,128)}, u32[]{:S(2)}) copy-start(f32[32,32,256]{2,1,0:T(8,128)} %c_ref.3) | copy-start | bytes 3145732
  13.3 7.5 %collective-permute-start.1 = (f32[4,32,256]{2,1,0:T(8,128)S(1)}, f32[4,32,256]{2,1,0:T(8,128)S(1)}, u32[]{:S(2)}, u32[]{:S(2)}) collective-permute-start(f32[4,32,256]{2,1,0:T(8,128)S(1)} %get-tuple-element.18), channel_id=1, source_target_pairs={{0,16},{16,32},{32,48},{48,64},{64,80},{80,96},{96,112},{112,128},... | collective-permute-start | bytes 393224 | tf_op jit(solution)/shard_map/ppermute | solution.py:333
  13.3 52.0 %copy-start.3 = (f32[32,32,256]{2,1,0:T(8,128)S(1)}, f32[32,32,256]{2,1,0:T(8,128)}, u32[]{:S(2)}) copy-start(f32[32,32,256]{2,1,0:T(8,128)} %param.6) | copy-start | bytes 3145732

commit v3 on v2

--- a/solution.py
+++ b/solution.py
@@ -1,4 +1,5 @@
 import functools
+import itertools
 
 import jax
 import jax.numpy as jnp
@@ -11,7 +12,7 @@
 LANES = 128
 SUB = 8
 MIB = 1 << 20
-MOST_VMEM = 66322432
+MOST_VMEM = 60817408
 f32 = jnp.float32
 
 
@@ -91,26 +92,25 @@
     ]
 
 
-def pack_kernel(field_hbm, weight_hbm, c_hbm, rows_ref, field_ref, weight_ref, c_ref, sem):
-    tile = pl.ds(field_hbm.shape[1] - SUB, SUB)
-    copies = [
-        pltpu.make_async_copy(hbm.at[:, tile, :], ref, sem.at[k])
-        for k, (hbm, ref) in enumerate(
-            ((field_hbm, field_ref), (weight_hbm, weight_ref), (c_hbm, c_ref))
-        )
-    ]
+def pack_kernel(ny, field_hbm, weight_hbm, c_hbm, rows_ref, sem):
+    nx, per_x = field_hbm.shape[0], field_hbm.shape[1]
+    halves = per_x // ny
+    copies = []
+    for k, (hbm, y) in enumerate(
+        ((field_hbm, ny - 1), (field_hbm, ny - 2), (weight_hbm, ny - 1), (c_hbm, ny - 1))
+    ):
+        for h in range(halves):
+            at = (y // SUB * halves + h) * SUB + y % SUB
+            place = k * halves + h
+            copies.append(
+                pltpu.make_async_copy(
+                    hbm.at[:, at], rows_ref.at[pl.ds(place * nx, nx)], sem.at[place]
+                )
+            )
     for copy in copies:
         copy.start()
     for copy in copies:
         copy.wait()
-    rows_ref[0] = field_ref[:, SUB - 1, :]
-    rows_ref[1] = field_ref[:, SUB - 2, :]
-    rows_ref[2] = weight_ref[:, SUB - 1, :]
-    rows_ref[3] = c_ref[:, SUB - 1, :]
-
-
-def stage_kernel(field_ref, weight_ref, c_ref, token_ref):
-    token_ref[...] = field_ref[0, 0:SUB, 0:LANES] + weight_ref[0, 0:SUB, 0:LANES] + c_ref[0, 0:SUB, 0:LANES]
 
 
 def not_first(axis):
@@ -119,8 +119,8 @@
 
 class Rows:
     def __init__(self, shape, rows_ref, inside):
-        self.n = shape[0]
-        self.row = lax.broadcasted_iota(jnp.int32, shape, 0)
+        self.nx, self.n = shape[:2]
+        self.row = lax.broadcasted_iota(jnp.int32, shape[1:], 0)
         self.rows_ref = rows_ref
         self.inside = inside
 
@@ -128,7 +128,9 @@
         return jnp.where(self.row == place, row, plane)
 
     def got(self, k, i):
-        return self.rows_ref[k, i : i + 1, :]
+        halves = self.row.shape[1] // LANES
+        at = [(k * halves + h) * self.nx + i for h in range(halves)]
+        return jnp.concatenate([self.rows_ref[r : r + 1, :] for r in at], axis=1)
 
     def plane(self, ref, k, i):
         return self.put(self.n - 1, self.got(k, i), ref[i])
@@ -143,68 +145,98 @@
         return up - self.put(n - 1, self.got(1, i), down)
 
 
-def matrix_x_kernel(
-    field_ref, weight_ref, c_ref, rows_ref, token_ref,
-    inv_ref, gam_ref, tau_ref, mat_ref, up_ref,
+def ahead_kernel(field_ref, weight_ref, c_ref, up_ref, corner_ref):
+    n, ny, _ = c_ref.shape
+    inside = not_first("gy")
+    row = lax.broadcasted_iota(jnp.int32, c_ref.shape[1:], 0)
+    edge = (row == 0) | (row == ny - 1)
+
+    def difference(plane):
+        up = pltpu.roll(plane, ny - 1, 0)
+        up = jnp.where(row == ny - 1, up * inside, up)
+        return up - jnp.where(edge, 0.0, pltpu.roll(plane, 1, 0))
+
+    last, before = field_ref[n - 1], field_ref[n - 2]
+    weight = weight_ref[n - 1] * 0.25
+    before_difference = difference(before)
+    up_ref[0] = difference(last)
+    up_ref[1] = jnp.where(row == ny - 1, before_difference, last - weight * before_difference)
+    up_ref[2] = weight
+    t = STEP * c_ref[0]
+    ground = jnp.ones_like(t)
+    for i in range(n - 1):
+        c = STEP * c_ref[i + 1]
+        gam = c / (t + ground + c)
+        ground = 1.0 + gam * ground
+        t = t * gam
+    ground = ground + t * (1.0 - not_first("gx"))
+    up_ref[3] = ground
+    for k, (plane, y) in enumerate(
+        ((last, -1), (last, -2), (before, -1), (before, -2), (weight, -1), (ground, -1))
+    ):
+        corner_ref[k : k + 1, :] = plane[ny + y : ny + y + 1, :]
+    corner_ref[6:8, :] = jnp.zeros_like(corner_ref[6:8, :])
+
+
+def forward_x_kernel(
+    field_ref, weight_ref, c_ref, rows_ref, up_ref, gam_ref, tau_ref, phi_ref, mat_ref, side_ref,
 ):
     n = c_ref.shape[0]
-    rows = Rows(c_ref.shape[1:], rows_ref, not_first("gy"))
-    up_ref[0] = rows.difference(field_ref, n - 1)
-    weight = rows.plane(weight_ref, 2, n - 1) * 0.25
-    before = rows.difference(field_ref, n - 2)
-    up_ref[1] = rows.plane(field_ref, 0, n - 1) - weight * before
-    up_ref[2] = weight
+    rows = Rows(c_ref.shape, rows_ref, not_first("gy"))
     left = STEP * rows.plane(c_ref, 3, 0)
     t = left
     a = jnp.zeros_like(t)
     ground = jnp.ones_like(t)
+    diffs = {-1: 0.0, 0: rows.difference(field_ref, 0)}
+    side_ref[3] = diffs[0]
+    q = j = 0.0
     for i in range(n - 1):
         c = STEP * rows.plane(c_ref, 3, i + 1)
         inv = 1.0 / (t + ground + c)
         gam = c * inv
         tau = t * inv
-        inv_ref[i] = inv
         gam_ref[i] = gam
         tau_ref[i] = tau
         a = a + tau * ground
         ground = 1.0 + gam * ground
         t = t * gam
-    up_ref[3] = ground + t * (1.0 - not_first("gx"))
-    for k, value in enumerate((t, a, left)):
-        mat_ref[k] = value
-
-
-def forward_x_kernel(
-    field_ref, weight_ref, rows_ref, inv_ref, gam_ref, tau_ref, phi_ref, side_ref,
-):
-    n = field_ref.shape[0]
-    rows = Rows(field_ref.shape[1:], rows_ref, not_first("gy"))
-    diffs = {-1: 0.0, 0: rows.difference(field_ref, 0)}
-    side_ref[3] = diffs[0]
-    q = j = 0.0
-    for i in range(n - 1):
         diffs[i + 1] = rows.difference(field_ref, i + 1)
         weight = rows.plane(weight_ref, 2, i) * 0.25
         if i == 0:
             side_ref[2] = weight
         h = rows.plane(field_ref, 0, i) + weight * (diffs[i + 1] - diffs.pop(i - 1)) + q
-        phi_ref[i] = inv_ref[i] * h
-        q = gam_ref[i] * h
-        j = j + tau_ref[i] * h
+        phi_ref[i] = inv * h
+        q = gam * h
+        j = j + tau * h
     side_ref[0] = j
     side_ref[1] = q
-
-
-def finish_x_kernel(got_ref, mat_ref, side_ref, buf_ref, extra_ref):
-    inside = not_first("gx")
+    for k, value in enumerate((t, a, left)):
+        mat_ref[k] = value
+
+
+def finish_x_kernel(got_ref, corner_ref, mat_ref, side_ref, buf_ref, extra_ref):
+    ny = got_ref.shape[1]
+    inside_x, inside_y = not_first("gx"), not_first("gy")
+    row = lax.broadcasted_iota(jnp.int32, got_ref.shape[1:], 0)
+    first, last = row == 0, row == ny - 1
+    f, f2, b, b2, w, ground = (corner_ref[k : k + 1, :] for k in range(6))
+    difference = got_ref[0] - jnp.where(first, f * inside_y, jnp.where(last, f2, 0.0))
+    weight = jnp.where(last, w, got_ref[2])
+    partial = got_ref[1]
+    partial = jnp.where(
+        last,
+        f - w * (partial - b2),
+        partial + jnp.where(first, weight * (b * inside_y), 0.0),
+    )
+    grounds = jnp.where(last, ground, got_ref[3])
     t, a, left = (mat_ref[k] for k in range(3))
-    f0 = side_ref[2] * got_ref[0] * -inside
+    f0 = side_ref[2] * difference * -inside_x
     extra = f0 / left
-    source = got_ref[1] + got_ref[2] * side_ref[3] * inside
-    j = (side_ref[0] + f0 - (a + t) * extra) * inside + source
+    source = partial + weight * side_ref[3] * inside_x
+    j = (side_ref[0] + f0 - (a + t) * extra) * inside_x + source
     q = side_ref[1] + t * extra
     extra_ref[...] = extra
-    store_values(buf_ref, [t * inside, got_ref[3] + a * inside, j, q])
+    store_values(buf_ref, [t * inside_x, grounds + a * inside_x, j, q])
 
 
 def solve_kernel(n, m, halves, count, in_ref, out_ref):
@@ -328,9 +360,18 @@
     )(*args)
 
 
-def from_before(value, axis):
-    n = lax.axis_size(axis)
-    return lax.ppermute(value, axis, [(i, (i + 1) % n) for i in range(n)])
+def from_before(value, *axes):
+    sizes = [lax.axis_size(axis) for axis in axes]
+
+    def index(place):
+        at = 0
+        for i, n in zip(place, sizes, strict=True):
+            at = at * n + i % n
+        return at
+
+    places = itertools.product(*(range(n) for n in sizes))
+    pairs = [(index(place), index([i + 1 for i in place])) for place in places]
+    return lax.ppermute(value, axes, pairs)
 
 
 def exchange(buf, axis):
@@ -355,25 +396,23 @@
     x_plane = (ny, nz)
     y_plane = (nx, nz)
     blocks = pltpu.SemaphoreType.DMA((ny // SUB,))
-    tile = pltpu.VMEM((nx, SUB, nz), f32)
+    single = [tile_rows(v).reshape(nx, ny * halves, 1, LANES) for v in (field, cross_weight, cond_x)]
     (rows,) = call(
-        pack_kernel, [field, cross_weight, cond_x], [(4, *y_plane)], "pack",
-        scratch=(tile, tile, tile, pltpu.SemaphoreType.DMA((3,))), hbm_args=(0, 1, 2),
-        limit=MOST_VMEM,
-    )
-    rows = from_before(rows, "gy")
-    (token,) = call(stage_kernel, [field, cross_weight, cond_x], [(SUB, LANES)], "stage")
-    inv_x, gam_x, tau_x, mat_x, up = call(
-        matrix_x_kernel, [field, cross_weight, cond_x, rows, token],
-        [(nx - 1, *x_plane)] * 3 + [(3, *x_plane), (4, *x_plane)], "matrix_x",
-    )
+        functools.partial(pack_kernel, ny), single, [(4 * halves * nx, 1, LANES)], "pack",
+        scratch=(pltpu.SemaphoreType.DMA((4 * halves,)),), hbm_args=(0, 1, 2), limit=MOST_VMEM,
+    )
+    rows = from_before(rows, "gy").reshape(4 * halves * nx, LANES)
+    up, corner = call(
+        ahead_kernel, [field, cross_weight, cond_x], [(4, *x_plane), (SUB, nz)], "ahead"
+    )
+    corner = from_before(corner, "gx", "gy")
     got = from_before(up, "gx")
-    phi_x, side = call(
-        forward_x_kernel, [field, cross_weight, rows, inv_x, gam_x, tau_x],
-        [(nx - 1, *x_plane), (4, *x_plane)], "forward_x", bytes_accessed=4 << 20,
+    gam_x, tau_x, phi_x, mat_x, side = call(
+        forward_x_kernel, [field, cross_weight, cond_x, rows, up],
+        [(nx - 1, *x_plane)] * 3 + [(3, *x_plane), (4, *x_plane)], "forward_x",
     )
     buf_x, extra = call(
-        finish_x_kernel, [got, mat_x, side], [(ny * 4 * halves, LANES), x_plane], "finish_x"
+        finish_x_kernel, [got, corner, mat_x, side], [(ny * 4 * halves, LANES), x_plane], "finish_x"
     )
     ends_x = interfaces(buf_x, "gx", ny, halves, 4)
     phi_y, gam_y, tau_y, buf_y = call(

time: 93.2 us -> 90.2 us (0.968)
  starting transfers between devices: 3.42 us -> 8.14 us
  waiting for transfers between devices: 10.7 us -> 6 us
  local copies, waits for them, and re-layouts: 3.67 us -> 0.01 us
    ppermute x2 -> x3, starting transfers between devices: 3.42 us -> 8.14 us  [from_before(): return lax.ppermute(value, axes, pairs)]
    ppermute x2 -> x3, waiting for transfers between devices: 10.7 us -> 6 us  [from_before(): return lax.ppermute(value, axes, pairs)]
    unnamed x8, local copies, waits for them, and re-layouts: 3.67 us -> 0.01 us
    pallas_call x9 -> x8, Pallas kernels: 5.92 us -> 6.19 us  [call(): pl.pallas_call(kernel, out_shape=[jax.ShapeDtypeStruct(s, f32) for s in o...]
  transfers between devices with their start and end apart: 2 -> 3, of which waited for: 2 -> 2; matrix products, arithmetic and copies ran while one was open for 0% -> 0% of each run, Pallas kernels for 1% -> 2%
where the time goes in v3:
time: 90.2 us; the launch traced here: 89.9 us
  blocking collectives  69.5 us (77%)
  starting transfers between devices  8.14 us (9%)
  Pallas kernels  6.19 us (7%)
  waiting for transfers between devices  6 us (7%)
    all_to_all x4, blocking collectives, exchange(): lax.all_to_all(buf.reshape(n, 1, rows * lanes // n), axis, 0, 0, tiled=True)  69.5 us
    ppermute x3, starting transfers between devices, from_before(): return lax.ppermute(value, axes, pairs)  8.14 us
    pallas_call x8, Pallas kernels, call(): pl.pallas_call(kernel, out_shape=[jax.ShapeDtypeStruct(s, f32) for s in o...  6.19 us
    ppermute x3, waiting for transfers between devices, from_before(): return lax.ppermute(value, axes, pairs)  6 us
  transfers between devices with their start and end apart: 3, of which 2 were waited for; matrix products, arithmetic and copies ran while one was open for 0% of the time, Pallas kernels for 2%

profile of v3, /device:TPU:2, one launch (start us, length us, event | category | flops | bytes accessed | tf_op | source)
XLA Modules:
  0.0 89.9 jit_solution(13001265051585547507)
XLA Ops:
  0.0 0.0 copy-start
  0.0 0.0 copy-start.1
  0.0 0.0 copy-start.2
  0.0 1.7 %pack.1 = f32[256,1,128]{2,1,0:T(1,128)} custom-call(f32[32,64,1,128]{3,2,1,0:T(1,128)} %bitcast.35, f32[32,64,1,128]{3,2,1,0:T(1,128)} %bitcast.36, f32[32,64,1,128]{3,2,1,0:T(1,128)} %bitcast.37), custom_call_target="tpu_custom_call" | custom-call | flops 1048576 | bytes 1048576 | tf_op jit(solution)/shard_map/pack/pallas_call | solution.py:351
  1.7 3.4 %collective-permute-start.2 = (f32[256,1,128]{2,0,1:T(8,128)}, f32[256,1,128]{2,0,1:T(8,128)S(1)}, u32[]{:S(2)}, u32[]{:S(2)}) collective-permute-start(f32[256,1,128]{2,0,1:T(8,128)} %bitcast.48), channel_id=1, source_target_pairs={{0,1},{1,2},{2,3},{3,4},{4,5},{5,6},{6,7},{7,8},{8,9},{9,10},{10,1... | collective-permute-start | bytes 393224 | tf_op jit(solution)/shard_map/ppermute | solution.py:374
  5.1 0.0 copy-done
  5.1 0.0 copy-done.1
  5.1 0.0 copy-done.2
  5.1 0.4 ahead.1
  5.5 0.0 collective-permute-start
  5.6 4.7 %collective-permute-start.1 = (f32[8,256]{1,0:T(8,128)S(1)}, f32[8,256]{1,0:T(8,128)S(1)}, u32[]{:S(2)}, u32[]{:S(2)}) collective-permute-start(f32[8,256]{1,0:T(8,128)S(1)} %get-tuple-element.19), channel_id=1, source_target_pairs={{0,17},{1,18},{2,19},{3,20},{4,21},{5,22},{6,23},{7,24},{8,25},{9,... | collective-permute-start | bytes 24584 | tf_op jit(solution)/shard_map/ppermute | solution.py:374
  10.3 2.4 %collective-permute-done.2 = f32[256,1,128]{2,0,1:T(8,128)S(1)} collective-permute-done((f32[256,1,128]{2,0,1:T(8,128)}, f32[256,1,128]{2,0,1:T(8,128)S(1)}, u32[]{:S(2)}, u32[]{:S(2)}) %collective-permute-start.2) | collective-permute-done | bytes 131104 | tf_op jit(solution)/shard_map/ppermute | solution.py:374
  12.6 0.0 copy-start.3
  12.6 1.1 %forward_x.1 = (f32[31,32,256]{2,1,0:T(8,128)S(1)}, f32[31,32,256]{2,1,0:T(8,128)S(1)}, f32[31,32,256]{2,1,0:T(8,128)S(1)}, f32[3,32,256]{2,1,0:T(8,128)S(1)}, f32[4,32,256]{2,1,0:T(8,128)S(1)}) custom-call(f32[32,32,256]{2,1,0:T(8,128)S(1)} %copy-done, f32[32,32,256]{2,1,0:T(8,128)S(1)} %copy-done.1, f32[32,32,256]{2,1,0:T(8,128)S(1)} %copy-done.2, ...), custom_call_target="tpu_custom_call" | custom-call | flops 1048576 | bytes 1048576 | tf_op jit(solution)/shard_map/forward_x/pallas_call | solution.py:351
  13.8 3.6 %collective-permute-done.1.corner_ref = f32[8,256]{1,0:T(8,128)S(1)} collective-permute-done((f32[8,256]{1,0:T(8,128)S(1)}, f32[8,256]{1,0:T(8,128)S(1)}, u32[]{:S(2)}, u32[]{:S(2)}) %collective-permute-start.1) | collective-permute-done | bytes 8224 | tf_op jit(solution)/shard_map/ppermute | solution.py:374
  17.4 0.0 collective-permute-done.got_ref
  17.5 27.7 %all_to_all.20 = f32[32,1,1024]{2,1,0:T(1,128)S(1)} all-to-all(f32[32,1,1024]{2,1,0:T(1,128)S(1)} %bitcast.46), channel_id=1, replica_groups=mesh['gx'=32,'gy'=16] {'gx'}, dimensions={0} | all-to-all | bytes 262144 | tf_op jit(solution)/shard_map/all_to_all | solution.py:380
  45.2 0.2 solve_gx.1
  45.3 17.3 %all_to_all.21 = f32[32,1,512]{2,1,0:T(1,128)S(1)} all-to-all(f32[32,1,512]{2,1,0:T(1,128)S(1)} %bitcast.43), channel_id=1, replica_groups=mesh['gx'=32,'gy'=16] {'gx'}, dimensions={0} | all-to-all | bytes 131072 | tf_op jit(solution)/shard_map/all_to_all | solution.py:380
  62.6 0.0 copy-done.3
  62.6 1.4 %middle.1 = (f32[31,32,256]{2,1,0:T(8,128)S(1)}, f32[31,32,256]{2,1,0:T(8,128)S(1)}, f32[31,32,256]{2,1,0:T(8,128)S(1)}, f32[320,128]{1,0:T(8,128)S(1)}) custom-call(f32[128,128]{1,0:T(8,128)S(1)} %bitcast.41, f32[32,256]{1,0:T(8,128)S(1)} %get-tuple-element.23.extra_ref, f32[31,32,256]{2,1,0:T(8,128)S(1)} %get-tuple-element.24.phi_x_ref, ...), custom_call_target="tpu_custom_call" | custom-call | flops 1048576 | bytes 1048576 | tf_op jit(solution)/shard_map/middle/pallas_call | solution.py:351
  64.0 13.8 %all_to_all.22 = f32[16,1,2560]{2,1,0:T(1,128)S(1)} all-to-all(f32[16,1,2560]{2,1,0:T(1,128)S(1)} %bitcast.45), channel_id=1, replica_groups=mesh['gx'=32,'gy'=16] {'gy'}, dimensions={0} | all-to-all | bytes 327680 | tf_op jit(solution)/shard_map/all_to_all | solution.py:380
  77.8 0.1 solve_gy.1
  78.0 10.7 %all_to_all.23 = f32[16,1,1024]{2,1,0:T(1,128)S(1)} all-to-all(f32[16,1,1024]{2,1,0:T(1,128)S(1)} %bitcast.44), channel_id=1, replica_groups=mesh['gx'=32,'gy'=16] {'gy'}, dimensions={0} | all-to-all | bytes 131072 | tf_op jit(solution)/shard_map/all_to_all | solution.py:380
  88.7 1.2 %backward_y.1 = f32[32,4,16,128]{3,2,1,0:T(8,128)} custom-call(f32[128,128]{1,0:T(8,128)S(1)} %bitcast.42, f32[31,32,256]{2,1,0:T(8,128)S(1)} %get-tuple-element.28.phi_ref, f32[31,32,256]{2,1,0:T(8,128)S(1)} %get-tuple-element.29.gam_ref, f32[31,32,256]{2,1,0:T(8,128)S(1)} %get-tuple-element.30.tau_ref), custom_call_target="tpu_custom_call" | custom-call | flops 1048576 | bytes 1048576 | tf_op jit(solution)/shard_map/backward_y/pallas_call | solution.py:351
  (1 shorter events, 0.0 us)
Async XLA Ops:
  0.0 5.1 %copy-start = (f32[32,32,256]{2,1,0:T(8,128)S(1)}, f32[32,32,256]{2,1,0:T(8,128)}, u32[]{:S(2)}) copy-start(f32[32,32,256]{2,1,0:T(8,128)} %field_ref.3) | copy-start | bytes 3145732
  0.0 5.1 %copy-start.1 = (f32[32,32,256]{2,1,0:T(8,128)S(1)}, f32[32,32,256]{2,1,0:T(8,128)}, u32[]{:S(2)}) copy-start(f32[32,32,256]{2,1,0:T(8,128)} %weight_ref.3) | copy-start | bytes 3145732
  0.0 5.1 %copy-start.2 = (f32[32,32,256]{2,1,0:T(8,128)S(1)}, f32[32,32,256]{2,1,0:T(8,128)}, u32[]{:S(2)}) copy-start(f32[32,32,256]{2,1,0:T(8,128)} %c_ref.3) | copy-start | bytes 3145732
  1.7 10.9 %collective-permute-start.2 = (f32[256,1,128]{2,0,1:T(8,128)}, f32[256,1,128]{2,0,1:T(8,128)S(1)}, u32[]{:S(2)}, u32[]{:S(2)}) collective-permute-start(f32[256,1,128]{2,0,1:T(8,128)} %bitcast.48), channel_id=1, source_target_pairs={{0,1},{1,2},{2,3},{3,4},{4,5},{5,6},{6,7},{7,8},{8,9},{9,10},{10,1... | collective-permute-start | bytes 393224 | tf_op jit(solution)/shard_map/ppermute | solution.py:374
  5.5 11.9 %collective-permute-start = (f32[4,32,256]{2,1,0:T(8,128)S(1)}, f32[4,32,256]{2,1,0:T(8,128)S(1)}, u32[]{:S(2)}, u32[]{:S(2)}) collective-permute-start(f32[4,32,256]{2,1,0:T(8,128)S(1)} %get-tuple-element.18.up_ref), channel_id=1, source_target_pairs={{0,16},{16,32},{32,48},{48,64},{64,80},{80,96},{96,112},{112,128},... | collective-permute-start | bytes 393224 | tf_op jit(solution)/shard_map/ppermute | solution.py:374
  5.6 11.9 %collective-permute-start.1 = (f32[8,256]{1,0:T(8,128)S(1)}, f32[8,256]{1,0:T(8,128)S(1)}, u32[]{:S(2)}, u32[]{:S(2)}) collective-permute-start(f32[8,256]{1,0:T(8,128)S(1)} %get-tuple-element.19), channel_id=1, source_target_pairs={{0,17},{1,18},{2,19},{3,20},{4,21},{5,22},{6,23},{7,24},{8,25},{9,... | collective-permute-start | bytes 24584 | tf_op jit(solution)/shard_map/ppermute | solution.py:374
  12.6 50.0 %copy-start.3 = (f32[32,32,256]{2,1,0:T(8,128)S(1)}, f32[32,32,256]{2,1,0:T(8,128)}, u32[]{:S(2)}) copy-start(f32[32,32,256]{2,1,0:T(8,128)} %param.6) | copy-start | bytes 3145732

commit v4 on v3

--- a/solution.py
+++ b/solution.py
@@ -12,7 +12,7 @@
 LANES = 128
 SUB = 8
 MIB = 1 << 20
-MOST_VMEM = 60817408
+MOST_VMEM = 55574528
 f32 = jnp.float32
 
 

time: 90.2 us -> 89.5 us (level)
  no operation moved by 1% of the time
where the time goes in v4:
time: 89.5 us; the launch traced here: 89.2 us
  blocking collectives  69.5 us (78%)
  starting transfers between devices  8.14 us (9%)
  waiting for transfers between devices  6 us (7%)
  Pallas kernels  5.53 us (6%)
    all_to_all x4, blocking collectives, exchange(): lax.all_to_all(buf.reshape(n, 1, rows * lanes // n), axis, 0, 0, tiled=True)  69.5 us
    ppermute x3, starting transfers between devices, from_before(): return lax.ppermute(value, axes, pairs)  8.14 us
    ppermute x3, waiting for transfers between devices, from_before(): return lax.ppermute(value, axes, pairs)  6 us
    pallas_call x8, Pallas kernels, call(): pl.pallas_call(kernel, out_shape=[jax.ShapeDtypeStruct(s, f32) for s in o...  5.53 us
  transfers between devices with their start and end apart: 3, of which 2 were waited for; matrix products, arithmetic and copies ran while one was open for 0% of the time, Pallas kernels for 2%

profile of v4, /device:TPU:2, one launch (start us, length us, event | category | flops | bytes accessed | tf_op | source)
XLA Modules:
  0.0 89.2 jit_solution(5046789879463471498)
XLA Ops:
  0.0 0.0 copy-start
  0.0 0.0 copy-start.1
  0.0 0.0 copy-start.2
  0.0 1.0 %pack.1 = f32[256,1,128]{2,1,0:T(1,128)S(1)} custom-call(f32[32,64,1,128]{3,2,1,0:T(1,128)} %bitcast.35, f32[32,64,1,128]{3,2,1,0:T(1,128)} %bitcast.36, f32[32,64,1,128]{3,2,1,0:T(1,128)} %bitcast.37), custom_call_target="tpu_custom_call" | custom-call | flops 1048576 | bytes 1048576 | tf_op jit(solution)/shard_map/pack/pallas_call | solution.py:351
  1.1 3.4 %collective-permute-start.2 = (f32[256,1,128]{2,0,1:T(8,128)S(1)}, f32[256,1,128]{2,0,1:T(8,128)S(1)}, u32[]{:S(2)}, u32[]{:S(2)}) collective-permute-start(f32[256,1,128]{2,0,1:T(8,128)S(1)} %bitcast.46), channel_id=1, source_target_pairs={{0,1},{1,2},{2,3},{3,4},{4,5},{5,6},{6,7},{7,8},{8,9},{9,10},{10,1... | collective-permute-start | bytes 393224 | tf_op jit(solution)/shard_map/ppermute | solution.py:374
  4.5 0.0 copy-done
  4.5 0.0 copy-done.1
  4.5 0.0 copy-done.2
  4.5 0.4 ahead.1
  4.9 0.0 collective-permute-start
  4.9 4.7 %collective-permute-start.1 = (f32[8,256]{1,0:T(8,128)S(1)}, f32[8,256]{1,0:T(8,128)S(1)}, u32[]{:S(2)}, u32[]{:S(2)}) collective-permute-start(f32[8,256]{1,0:T(8,128)S(1)} %get-tuple-element.19), channel_id=1, source_target_pairs={{0,17},{1,18},{2,19},{3,20},{4,21},{5,22},{6,23},{7,24},{8,25},{9,... | collective-permute-start | bytes 24584 | tf_op jit(solution)/shard_map/ppermute | solution.py:374
  9.6 2.1 %collective-permute-done.2 = f32[256,1,128]{2,0,1:T(8,128)S(1)} collective-permute-done((f32[256,1,128]{2,0,1:T(8,128)S(1)}, f32[256,1,128]{2,0,1:T(8,128)S(1)}, u32[]{:S(2)}, u32[]{:S(2)}) %collective-permute-start.2) | collective-permute-done | bytes 131104 | tf_op jit(solution)/shard_map/ppermute | solution.py:374
  11.8 0.0 copy-start.3
  11.8 1.1 %forward_x.1 = (f32[31,32,256]{2,1,0:T(8,128)S(1)}, f32[31,32,256]{2,1,0:T(8,128)S(1)}, f32[31,32,256]{2,1,0:T(8,128)S(1)}, f32[3,32,256]{2,1,0:T(8,128)S(1)}, f32[4,32,256]{2,1,0:T(8,128)S(1)}) custom-call(f32[32,32,256]{2,1,0:T(8,128)S(1)} %copy-done, f32[32,32,256]{2,1,0:T(8,128)S(1)} %copy-done.1, f32[32,32,256]{2,1,0:T(8,128)S(1)} %copy-done.2, ...), custom_call_target="tpu_custom_call" | custom-call | flops 1048576 | bytes 1048576 | tf_op jit(solution)/shard_map/forward_x/pallas_call | solution.py:351
  12.9 3.9 %collective-permute-done.1.corner_ref = f32[8,256]{1,0:T(8,128)S(1)} collective-permute-done((f32[8,256]{1,0:T(8,128)S(1)}, f32[8,256]{1,0:T(8,128)S(1)}, u32[]{:S(2)}, u32[]{:S(2)}) %collective-permute-start.1) | collective-permute-done | bytes 8224 | tf_op jit(solution)/shard_map/ppermute | solution.py:374
  16.8 0.0 collective-permute-done.got_ref
  16.8 27.7 %all_to_all.20 = f32[32,1,1024]{2,1,0:T(1,128)S(1)} all-to-all(f32[32,1,1024]{2,1,0:T(1,128)S(1)} %bitcast.47), channel_id=1, replica_groups=mesh['gx'=32,'gy'=16] {'gx'}, dimensions={0} | all-to-all | bytes 262144 | tf_op jit(solution)/shard_map/all_to_all | solution.py:380
  44.5 0.2 solve_gx.1
  44.7 17.3 %all_to_all.21 = f32[32,1,512]{2,1,0:T(1,128)S(1)} all-to-all(f32[32,1,512]{2,1,0:T(1,128)S(1)} %bitcast.43), channel_id=1, replica_groups=mesh['gx'=32,'gy'=16] {'gx'}, dimensions={0} | all-to-all | bytes 131072 | tf_op jit(solution)/shard_map/all_to_all | solution.py:380
  62.0 0.0 copy-done.3
  62.0 1.4 %middle.1 = (f32[31,32,256]{2,1,0:T(8,128)S(1)}, f32[31,32,256]{2,1,0:T(8,128)S(1)}, f32[31,32,256]{2,1,0:T(8,128)S(1)}, f32[320,128]{1,0:T(8,128)S(1)}) custom-call(f32[128,128]{1,0:T(8,128)S(1)} %bitcast.41, f32[32,256]{1,0:T(8,128)S(1)} %get-tuple-element.23.extra_ref, f32[31,32,256]{2,1,0:T(8,128)S(1)} %get-tuple-element.24.phi_x_ref, ...), custom_call_target="tpu_custom_call" | custom-call | flops 1048576 | bytes 1048576 | tf_op jit(solution)/shard_map/middle/pallas_call | solution.py:351
  63.4 13.8 %all_to_all.22 = f32[16,1,2560]{2,1,0:T(1,128)S(1)} all-to-all(f32[16,1,2560]{2,1,0:T(1,128)S(1)} %bitcast.45), channel_id=1, replica_groups=mesh['gx'=32,'gy'=16] {'gy'}, dimensions={0} | all-to-all | bytes 327680 | tf_op jit(solution)/shard_map/all_to_all | solution.py:380
  77.2 0.1 solve_gy.1
  77.3 10.7 %all_to_all.23 = f32[16,1,1024]{2,1,0:T(1,128)S(1)} all-to-all(f32[16,1,1024]{2,1,0:T(1,128)S(1)} %bitcast.44), channel_id=1, replica_groups=mesh['gx'=32,'gy'=16] {'gy'}, dimensions={0} | all-to-all | bytes 131072 | tf_op jit(solution)/shard_map/all_to_all | solution.py:380
  88.0 1.2 %backward_y.1 = f32[32,4,16,128]{3,2,1,0:T(8,128)} custom-call(f32[128,128]{1,0:T(8,128)S(1)} %bitcast.42, f32[31,32,256]{2,1,0:T(8,128)S(1)} %get-tuple-element.28.phi_ref, f32[31,32,256]{2,1,0:T(8,128)S(1)} %get-tuple-element.29.gam_ref, f32[31,32,256]{2,1,0:T(8,128)S(1)} %get-tuple-element.30.tau_ref), custom_call_target="tpu_custom_call" | custom-call | flops 1048576 | bytes 1048576 | tf_op jit(solution)/shard_map/backward_y/pallas_call | solution.py:351
  (1 shorter events, 0.0 us)
Async XLA Ops:
  0.0 4.5 %copy-start = (f32[32,32,256]{2,1,0:T(8,128)S(1)}, f32[32,32,256]{2,1,0:T(8,128)}, u32[]{:S(2)}) copy-start(f32[32,32,256]{2,1,0:T(8,128)} %field_ref.3) | copy-start | bytes 3145732
  0.0 4.5 %copy-start.1 = (f32[32,32,256]{2,1,0:T(8,128)S(1)}, f32[32,32,256]{2,1,0:T(8,128)}, u32[]{:S(2)}) copy-start(f32[32,32,256]{2,1,0:T(8,128)} %weight_ref.3) | copy-start | bytes 3145732
  0.0 4.5 %copy-start.2 = (f32[32,32,256]{2,1,0:T(8,128)S(1)}, f32[32,32,256]{2,1,0:T(8,128)}, u32[]{:S(2)}) copy-start(f32[32,32,256]{2,1,0:T(8,128)} %c_ref.3) | copy-start | bytes 3145732
  1.1 10.7 %collective-permute-start.2 = (f32[256,1,128]{2,0,1:T(8,128)S(1)}, f32[256,1,128]{2,0,1:T(8,128)S(1)}, u32[]{:S(2)}, u32[]{:S(2)}) collective-permute-start(f32[256,1,128]{2,0,1:T(8,128)S(1)} %bitcast.46), channel_id=1, source_target_pairs={{0,1},{1,2},{2,3},{3,4},{4,5},{5,6},{6,7},{7,8},{8,9},{9,10},{10,1... | collective-permute-start | bytes 393224 | tf_op jit(solution)/shard_map/ppermute | solution.py:374
  4.9 11.9 %collective-permute-start = (f32[4,32,256]{2,1,0:T(8,128)S(1)}, f32[4,32,256]{2,1,0:T(8,128)S(1)}, u32[]{:S(2)}, u32[]{:S(2)}) collective-permute-start(f32[4,32,256]{2,1,0:T(8,128)S(1)} %get-tuple-element.18.up_ref), channel_id=1, source_target_pairs={{0,16},{16,32},{32,48},{48,64},{64,80},{80,96},{96,112},{112,128},... | collective-permute-start | bytes 393224 | tf_op jit(solution)/shard_map/ppermute | solution.py:374
  4.9 11.9 %collective-permute-start.1 = (f32[8,256]{1,0:T(8,128)S(1)}, f32[8,256]{1,0:T(8,128)S(1)}, u32[]{:S(2)}, u32[]{:S(2)}) collective-permute-start(f32[8,256]{1,0:T(8,128)S(1)} %get-tuple-element.19), channel_id=1, source_target_pairs={{0,17},{1,18},{2,19},{3,20},{4,21},{5,22},{6,23},{7,24},{8,25},{9,... | collective-permute-start | bytes 24584 | tf_op jit(solution)/shard_map/ppermute | solution.py:374
  11.8 50.2 %copy-start.3 = (f32[32,32,256]{2,1,0:T(8,128)S(1)}, f32[32,32,256]{2,1,0:T(8,128)}, u32[]{:S(2)}) copy-start(f32[32,32,256]{2,1,0:T(8,128)} %param.6) | copy-start | bytes 3145732

commit v5 on v4

--- a/solution.py
+++ b/solution.py
@@ -10,6 +10,7 @@
 
 STEP = 16384.0
 LANES = 128
+SPARE = 8
 SUB = 8
 MIB = 1 << 20
 MOST_VMEM = 55574528
@@ -30,12 +31,12 @@
 
 def y_scratch(shape):
     nx, ny, nz = shape
-    return pltpu.VMEM((ny // SUB, nx * nz * SUB // LANES, LANES), f32)
+    return pltpu.VMEM((ny // SUB, nx * (nz * SUB // LANES + SPARE), LANES), f32)
 
 
 def y_rows(shape, y, h):
     nx, _, nz = shape
-    return y // SUB, pl.ds(h * SUB + y % SUB, nx, stride=SUB * nz // LANES), slice(None)
+    return y // SUB, pl.ds(h * SUB + y % SUB, nx, stride=SUB * nz // LANES + SPARE), slice(None)
 
 
 def load_y(ref, shape, y):
@@ -61,14 +62,15 @@
     halves = nz // LANES
     for yb in range(ny // SUB):
         for h in range(halves):
-            start = (x * halves + h) * SUB
+            start = x * (halves * SUB + SPARE) + h * SUB
             ref[yb, start : start + SUB, :] = value[
                 yb * SUB : (yb + 1) * SUB, h * LANES : (h + 1) * LANES
             ]
 
 
 def y_block_out(scratch, hbm, yb, sem):
-    block = scratch.at[yb].reshape(hbm.shape[0], hbm.shape[2], LANES)
+    rows = hbm.shape[2]
+    block = scratch.at[yb].reshape(hbm.shape[0], rows + SPARE, LANES).at[:, pl.ds(0, rows)]
     return pltpu.make_async_copy(block, hbm.at[:, yb], sem.at[yb])
 
 
@@ -214,7 +216,7 @@
         mat_ref[k] = value
 
 
-def finish_x_kernel(got_ref, corner_ref, mat_ref, side_ref, buf_ref, extra_ref):
+def finish_x_kernel(got_ref, corner_ref, mat_ref, side_ref, turned_ref, buf_ref, extra_ref):
     ny = got_ref.shape[1]
     inside_x, inside_y = not_first("gx"), not_first("gy")
     row = lax.broadcasted_iota(jnp.int32, got_ref.shape[1:], 0)
@@ -295,6 +297,11 @@
         emit(i, u)
 
 
+def turn_kernel(shape, c_ref, out_ref):
+    for y in range(shape[1]):
+        out_ref[y] = STEP * load_y_whole(c_ref, shape, y)
+
+
 def middle_kernel(
     shape, ends_ref, extra_ref, phi_x_ref, gam_x_ref, tau_x_ref, c_ref,
     phi_ref, gam_ref, tau_ref, buf_ref, half_ref,
@@ -303,12 +310,12 @@
     u_prev, u_own = load_values(ends_ref, ny, 2, nz // LANES)
     backward(nx, u_prev * not_first("gx") + extra_ref[...], u_own, gam_x_ref, tau_x_ref, phi_x_ref,
              lambda i, u: store_plane(half_ref, shape, i, u))
-    t = STEP * load_y_whole(c_ref, shape, 0)
+    t = c_ref[0]
     a = jnp.zeros_like(t)
     ground = jnp.ones_like(t)
     q = j = 0.0
     for y in range(ny - 1):
-        c = STEP * load_y_whole(c_ref, shape, y + 1)
+        c = c_ref[y + 1]
         h = load_y(half_ref, shape, y) + q
         inv = 1.0 / (t + ground + c)
         gam = c * inv
@@ -411,13 +418,17 @@
         forward_x_kernel, [field, cross_weight, cond_x, rows, up],
         [(nx - 1, *x_plane)] * 3 + [(3, *x_plane), (4, *x_plane)], "forward_x",
     )
+    (turned,) = call(
+        functools.partial(turn_kernel, shape), [tile_rows(cond_y)], [(ny, *y_plane)], "turn"
+    )
     buf_x, extra = call(
-        finish_x_kernel, [got, corner, mat_x, side], [(ny * 4 * halves, LANES), x_plane], "finish_x"
+        finish_x_kernel, [got, corner, mat_x, side, turned],
+        [(ny * 4 * halves, LANES), x_plane], "finish_x",
     )
     ends_x = interfaces(buf_x, "gx", ny, halves, 4)
     phi_y, gam_y, tau_y, buf_y = call(
         functools.partial(middle_kernel, shape),
-        [ends_x, extra, phi_x, gam_x, tau_x, tile_rows(cond_y)],
+        [ends_x, extra, phi_x, gam_x, tau_x, turned],
         [(ny - 1, *y_plane)] * 3 + [(nx * 5 * halves, LANES)], "middle",
         scratch=(y_scratch(shape),),
     )

time: 89.5 us -> 89 us (level)
    pallas_call x8 -> x9, Pallas kernels: 5.53 us -> 5.52 us  [call(): pl.pallas_call(kernel, out_shape=[jax.ShapeDtypeStruct(s, f32) for s in o...]
where the time goes in v5:
time: 89 us; the launch traced here: 88.7 us
  blocking collectives  69.5 us (78%)
  starting transfers between devices  8.27 us (9%)
  Pallas kernels  5.52 us (6%)
  waiting for transfers between devices  5.32 us (6%)
    all_to_all x4, blocking collectives, exchange(): lax.all_to_all(buf.reshape(n, 1, rows * lanes // n), axis, 0, 0, tiled=True)  69.5 us
    ppermute x3, starting transfers between devices, from_before(): return lax.ppermute(value, axes, pairs)  8.27 us
    pallas_call x9, Pallas kernels, call(): pl.pallas_call(kernel, out_shape=[jax.ShapeDtypeStruct(s, f32) for s in o...  5.52 us
    ppermute x3, waiting for transfers between devices, from_before(): return lax.ppermute(value, axes, pairs)  5.32 us
  transfers between devices with their start and end apart: 3, of which 2 were waited for; matrix products, arithmetic and copies ran while one was open for 0% of the time, Pallas kernels for 2%

profile of v5, /device:TPU:2, one launch (start us, length us, event | category | flops | bytes accessed | tf_op | source)
XLA Modules:
  0.0 88.7 jit_solution(8734570469294396752)
XLA Ops:
  0.0 0.0 copy-start
  0.0 0.0 copy-start.1
  0.0 0.0 copy-start.2
  0.0 1.0 %pack.1 = f32[256,1,128]{2,1,0:T(1,128)S(1)} custom-call(f32[32,64,1,128]{3,2,1,0:T(1,128)} %bitcast.35, f32[32,64,1,128]{3,2,1,0:T(1,128)} %bitcast.36, f32[32,64,1,128]{3,2,1,0:T(1,128)} %bitcast.37), custom_call_target="tpu_custom_call" | custom-call | flops 1048576 | bytes 1048576 | tf_op jit(solution)/shard_map/pack/pallas_call | solution.py:358
  1.1 0.0 copy-start.3
  1.1 3.5 %collective-permute-start.2 = (f32[256,1,128]{2,0,1:T(8,128)S(1)}, f32[256,1,128]{2,0,1:T(8,128)S(1)}, u32[]{:S(2)}, u32[]{:S(2)}) collective-permute-start(f32[256,1,128]{2,0,1:T(8,128)S(1)} %bitcast.46), channel_id=1, source_target_pairs={{0,1},{1,2},{2,3},{3,4},{4,5},{5,6},{6,7},{7,8},{8,9},{9,10},{10,1... | collective-permute-start | bytes 393224 | tf_op jit(solution)/shard_map/ppermute | solution.py:381
  4.6 0.0 copy-done
  4.6 0.0 copy-done.1
  4.6 0.0 copy-done.2
  4.6 0.4 ahead.1
  5.0 0.0 collective-permute-start
  5.0 4.7 %collective-permute-start.1 = (f32[8,256]{1,0:T(8,128)S(1)}, f32[8,256]{1,0:T(8,128)S(1)}, u32[]{:S(2)}, u32[]{:S(2)}) collective-permute-start(f32[8,256]{1,0:T(8,128)S(1)} %get-tuple-element.19), channel_id=1, source_target_pairs={{0,17},{1,18},{2,19},{3,20},{4,21},{5,22},{6,23},{7,24},{8,25},{9,... | collective-permute-start | bytes 24584 | tf_op jit(solution)/shard_map/ppermute | solution.py:381
  9.8 0.0 copy-done.3
  9.8 0.7 turn.1.turned_ref.c_ref
  10.5 1.5 %collective-permute-done.2 = f32[256,1,128]{2,0,1:T(8,128)S(1)} collective-permute-done((f32[256,1,128]{2,0,1:T(8,128)S(1)}, f32[256,1,128]{2,0,1:T(8,128)S(1)}, u32[]{:S(2)}, u32[]{:S(2)}) %collective-permute-start.2) | collective-permute-done | bytes 131104 | tf_op jit(solution)/shard_map/ppermute | solution.py:381
  11.9 1.1 %forward_x.1 = (f32[31,32,256]{2,1,0:T(8,128)S(1)}, f32[31,32,256]{2,1,0:T(8,128)S(1)}, f32[31,32,256]{2,1,0:T(8,128)S(1)}, f32[3,32,256]{2,1,0:T(8,128)S(1)}, f32[4,32,256]{2,1,0:T(8,128)S(1)}) custom-call(f32[32,32,256]{2,1,0:T(8,128)S(1)} %copy-done, f32[32,32,256]{2,1,0:T(8,128)S(1)} %copy-done.1, f32[32,32,256]{2,1,0:T(8,128)S(1)} %copy-done.2, ...), custom_call_target="tpu_custom_call" | custom-call | flops 1048576 | bytes 1048576 | tf_op jit(solution)/shard_map/forward_x/pallas_call | solution.py:358
  13.0 3.9 %collective-permute-done.1.corner_ref = f32[8,256]{1,0:T(8,128)S(1)} collective-permute-done((f32[8,256]{1,0:T(8,128)S(1)}, f32[8,256]{1,0:T(8,128)S(1)}, u32[]{:S(2)}, u32[]{:S(2)}) %collective-permute-start.1) | collective-permute-done | bytes 8224 | tf_op jit(solution)/shard_map/ppermute | solution.py:381
  16.9 0.0 collective-permute-done.got_ref
  17.0 27.7 %all_to_all.20 = f32[32,1,1024]{2,1,0:T(1,128)S(1)} all-to-all(f32[32,1,1024]{2,1,0:T(1,128)S(1)} %bitcast.47), channel_id=1, replica_groups=mesh['gx'=32,'gy'=16] {'gx'}, dimensions={0} | all-to-all | bytes 262144 | tf_op jit(solution)/shard_map/all_to_all | solution.py:387
  44.6 0.2 solve_gx.1
  44.8 17.3 %all_to_all.21 = f32[32,1,512]{2,1,0:T(1,128)S(1)} all-to-all(f32[32,1,512]{2,1,0:T(1,128)S(1)} %bitcast.43), channel_id=1, replica_groups=mesh['gx'=32,'gy'=16] {'gx'}, dimensions={0} | all-to-all | bytes 131072 | tf_op jit(solution)/shard_map/all_to_all | solution.py:387
  62.1 0.9 middle.1
  63.0 13.8 %all_to_all.22 = f32[16,1,2560]{2,1,0:T(1,128)S(1)} all-to-all(f32[16,1,2560]{2,1,0:T(1,128)S(1)} %bitcast.45), channel_id=1, replica_groups=mesh['gx'=32,'gy'=16] {'gy'}, dimensions={0} | all-to-all | bytes 327680 | tf_op jit(solution)/shard_map/all_to_all | solution.py:387
  76.8 0.1 solve_gy.1
  76.9 10.7 %all_to_all.23 = f32[16,1,1024]{2,1,0:T(1,128)S(1)} all-to-all(f32[16,1,1024]{2,1,0:T(1,128)S(1)} %bitcast.44), channel_id=1, replica_groups=mesh['gx'=32,'gy'=16] {'gy'}, dimensions={0} | all-to-all | bytes 131072 | tf_op jit(solution)/shard_map/all_to_all | solution.py:387
  87.6 1.1 %backward_y.1 = f32[32,4,16,128]{3,2,1,0:T(8,128)} custom-call(f32[128,128]{1,0:T(8,128)S(1)} %bitcast.42, f32[31,32,256]{2,1,0:T(8,128)S(1)} %get-tuple-element.28.phi_ref, f32[31,32,256]{2,1,0:T(8,128)S(1)} %get-tuple-element.29.gam_ref, f32[31,32,256]{2,1,0:T(8,128)S(1)} %get-tuple-element.30.tau_ref), custom_call_target="tpu_custom_call" | custom-call | flops 1048576 | bytes 1048576 | tf_op jit(solution)/shard_map/backward_y/pallas_call | solution.py:358
  (1 shorter events, 0.0 us)
Async XLA Ops:
  0.0 4.6 %copy-start = (f32[32,32,256]{2,1,0:T(8,128)S(1)}, f32[32,32,256]{2,1,0:T(8,128)}, u32[]{:S(2)}) copy-start(f32[32,32,256]{2,1,0:T(8,128)} %field_ref.3) | copy-start | bytes 3145732
  0.0 4.6 %copy-start.1 = (f32[32,32,256]{2,1,0:T(8,128)S(1)}, f32[32,32,256]{2,1,0:T(8,128)}, u32[]{:S(2)}) copy-start(f32[32,32,256]{2,1,0:T(8,128)} %weight_ref.3) | copy-start | bytes 3145732
  0.0 4.6 %copy-start.2 = (f32[32,32,256]{2,1,0:T(8,128)S(1)}, f32[32,32,256]{2,1,0:T(8,128)}, u32[]{:S(2)}) copy-start(f32[32,32,256]{2,1,0:T(8,128)} %c_ref.3) | copy-start | bytes 3145732
  1.1 8.7 %copy-start.3 = (f32[32,32,256]{2,1,0:T(8,128)S(1)}, f32[32,32,256]{2,1,0:T(8,128)}, u32[]{:S(2)}) copy-start(f32[32,32,256]{2,1,0:T(8,128)} %param.6) | copy-start | bytes 3145732
  1.1 10.9 %collective-permute-start.2 = (f32[256,1,128]{2,0,1:T(8,128)S(1)}, f32[256,1,128]{2,0,1:T(8,128)S(1)}, u32[]{:S(2)}, u32[]{:S(2)}) collective-permute-start(f32[256,1,128]{2,0,1:T(8,128)S(1)} %bitcast.46), channel_id=1, source_target_pairs={{0,1},{1,2},{2,3},{3,4},{4,5},{5,6},{6,7},{7,8},{8,9},{9,10},{10,1... | collective-permute-start | bytes 393224 | tf_op jit(solution)/shard_map/ppermute | solution.py:381
  5.0 11.9 %collective-permute-start = (f32[4,32,256]{2,1,0:T(8,128)S(1)}, f32[4,32,256]{2,1,0:T(8,128)S(1)}, u32[]{:S(2)}, u32[]{:S(2)}) collective-permute-start(f32[4,32,256]{2,1,0:T(8,128)S(1)} %get-tuple-element.18.up_ref), channel_id=1, source_target_pairs={{0,16},{16,32},{32,48},{48,64},{64,80},{80,96},{96,112},{112,128},... | collective-permute-start | bytes 393224 | tf_op jit(solution)/shard_map/ppermute | solution.py:381
  5.0 11.9 %collective-permute-start.1 = (f32[8,256]{1,0:T(8,128)S(1)}, f32[8,256]{1,0:T(8,128)S(1)}, u32[]{:S(2)}, u32[]{:S(2)}) collective-permute-start(f32[8,256]{1,0:T(8,128)S(1)} %get-tuple-element.19), channel_id=1, source_target_pairs={{0,17},{1,18},{2,19},{3,20},{4,21},{5,22},{6,23},{7,24},{8,25},{9,... | collective-permute-start | bytes 24584 | tf_op jit(solution)/shard_map/ppermute | solution.py:381

commit v6 on v5

--- a/solution.py
+++ b/solution.py
@@ -166,10 +166,12 @@
     up_ref[2] = weight
     t = STEP * c_ref[0]
     ground = jnp.ones_like(t)
+    both = t + ground
     for i in range(n - 1):
         c = STEP * c_ref[i + 1]
-        gam = c / (t + ground + c)
+        gam = c / (both + c)
         ground = 1.0 + gam * ground
+        both = 1.0 + gam * both
         t = t * gam
     ground = ground + t * (1.0 - not_first("gx"))
     up_ref[3] = ground
@@ -189,18 +191,20 @@
     t = left
     a = jnp.zeros_like(t)
     ground = jnp.ones_like(t)
+    both = t + ground
     diffs = {-1: 0.0, 0: rows.difference(field_ref, 0)}
     side_ref[3] = diffs[0]
     q = j = 0.0
     for i in range(n - 1):
         c = STEP * rows.plane(c_ref, 3, i + 1)
-        inv = 1.0 / (t + ground + c)
+        inv = 1.0 / (both + c)
         gam = c * inv
         tau = t * inv
         gam_ref[i] = gam
         tau_ref[i] = tau
         a = a + tau * ground
         ground = 1.0 + gam * ground
+        both = 1.0 + gam * both
         t = t * gam
         diffs[i + 1] = rows.difference(field_ref, i + 1)
         weight = rows.plane(weight_ref, 2, i) * 0.25
@@ -313,11 +317,12 @@
     t = c_ref[0]
     a = jnp.zeros_like(t)
     ground = jnp.ones_like(t)
+    both = t + ground
     q = j = 0.0
     for y in range(ny - 1):
         c = c_ref[y + 1]
         h = load_y(half_ref, shape, y) + q
-        inv = 1.0 / (t + ground + c)
+        inv = 1.0 / (both + c)
         gam = c * inv
         tau = t * inv
         phi_ref[y] = inv * h
@@ -327,6 +332,7 @@
         j = j + tau * h
         a = a + tau * ground
         ground = 1.0 + gam * ground
+        both = 1.0 + gam * both
         t = t * gam
     inside = not_first("gy")
     j = j * inside + load_y(half_ref, shape, ny - 1)

time: 89 us -> 89.1 us (level)
  transfers between devices with their start and end apart: 3 -> 3, of which waited for: 2 -> 2; matrix products, arithmetic and copies ran while one was open for 0% -> 0% of each run, Pallas kernels for 2% -> 3%
where the time goes in v6:
time: 89.1 us; the launch traced here: 88.8 us
  blocking collectives  69.5 us (78%)
  starting transfers between devices  8.27 us (9%)
  Pallas kernels  5.68 us (6%)
  waiting for transfers between devices  5.27 us (6%)
    all_to_all x4, blocking collectives, exchange(): lax.all_to_all(buf.reshape(n, 1, rows * lanes // n), axis, 0, 0, tiled=True)  69.5 us
    ppermute x3, starting transfers between devices, from_before(): return lax.ppermute(value, axes, pairs)  8.27 us
    pallas_call x9, Pallas kernels, call(): pl.pallas_call(kernel, out_shape=[jax.ShapeDtypeStruct(s, f32) for s in o...  5.68 us
    ppermute x3, waiting for transfers between devices, from_before(): return lax.ppermute(value, axes, pairs)  5.27 us
  transfers between devices with their start and end apart: 3, of which 2 were waited for; matrix products, arithmetic and copies ran while one was open for 0% of the time, Pallas kernels for 3%

profile of v6, /device:TPU:2, one launch (start us, length us, event | category | flops | bytes accessed | tf_op | source)
XLA Modules:
  0.0 88.8 jit_solution(17078764818921542741)
XLA Ops:
  0.0 0.0 copy-start
  0.0 0.0 copy-start.1
  0.0 0.0 copy-start.2
  0.0 1.0 %pack.1 = f32[256,1,128]{2,1,0:T(1,128)S(1)} custom-call(f32[32,64,1,128]{3,2,1,0:T(1,128)} %bitcast.35, f32[32,64,1,128]{3,2,1,0:T(1,128)} %bitcast.36, f32[32,64,1,128]{3,2,1,0:T(1,128)} %bitcast.37), custom_call_target="tpu_custom_call" | custom-call | flops 1048576 | bytes 1048576 | tf_op jit(solution)/shard_map/pack/pallas_call | solution.py:364
  1.1 0.0 copy-start.3
  1.1 3.5 %collective-permute-start.2 = (f32[256,1,128]{2,0,1:T(8,128)S(1)}, f32[256,1,128]{2,0,1:T(8,128)S(1)}, u32[]{:S(2)}, u32[]{:S(2)}) collective-permute-start(f32[256,1,128]{2,0,1:T(8,128)S(1)} %bitcast.46), channel_id=1, source_target_pairs={{0,1},{1,2},{2,3},{3,4},{4,5},{5,6},{6,7},{7,8},{8,9},{9,10},{10,1... | collective-permute-start | bytes 393224 | tf_op jit(solution)/shard_map/ppermute | solution.py:387
  4.6 0.0 copy-done
  4.6 0.0 copy-done.1
  4.6 0.0 copy-done.2
  4.6 0.5 ahead.1
  5.1 0.0 collective-permute-start
  5.2 4.7 %collective-permute-start.1 = (f32[8,256]{1,0:T(8,128)S(1)}, f32[8,256]{1,0:T(8,128)S(1)}, u32[]{:S(2)}, u32[]{:S(2)}) collective-permute-start(f32[8,256]{1,0:T(8,128)S(1)} %get-tuple-element.19), channel_id=1, source_target_pairs={{0,17},{1,18},{2,19},{3,20},{4,21},{5,22},{6,23},{7,24},{8,25},{9,... | collective-permute-start | bytes 24584 | tf_op jit(solution)/shard_map/ppermute | solution.py:387
  9.9 0.0 copy-done.3
  9.9 0.7 turn.1.turned_ref.c_ref
  10.6 1.3 %collective-permute-done.2 = f32[256,1,128]{2,0,1:T(8,128)S(1)} collective-permute-done((f32[256,1,128]{2,0,1:T(8,128)S(1)}, f32[256,1,128]{2,0,1:T(8,128)S(1)}, u32[]{:S(2)}, u32[]{:S(2)}) %collective-permute-start.2) | collective-permute-done | bytes 131104 | tf_op jit(solution)/shard_map/ppermute | solution.py:387
  11.9 1.2 %forward_x.1 = (f32[31,32,256]{2,1,0:T(8,128)S(1)}, f32[31,32,256]{2,1,0:T(8,128)S(1)}, f32[31,32,256]{2,1,0:T(8,128)S(1)}, f32[3,32,256]{2,1,0:T(8,128)S(1)}, f32[4,32,256]{2,1,0:T(8,128)S(1)}) custom-call(f32[32,32,256]{2,1,0:T(8,128)S(1)} %copy-done, f32[32,32,256]{2,1,0:T(8,128)S(1)} %copy-done.1, f32[32,32,256]{2,1,0:T(8,128)S(1)} %copy-done.2, ...), custom_call_target="tpu_custom_call" | custom-call | flops 1048576 | bytes 1048576 | tf_op jit(solution)/shard_map/forward_x/pallas_call | solution.py:364
  13.1 3.9 %collective-permute-done.1.corner_ref = f32[8,256]{1,0:T(8,128)S(1)} collective-permute-done((f32[8,256]{1,0:T(8,128)S(1)}, f32[8,256]{1,0:T(8,128)S(1)}, u32[]{:S(2)}, u32[]{:S(2)}) %collective-permute-start.1) | collective-permute-done | bytes 8224 | tf_op jit(solution)/shard_map/ppermute | solution.py:387
  17.0 0.0 collective-permute-done.got_ref
  17.1 27.7 %all_to_all.20 = f32[32,1,1024]{2,1,0:T(1,128)S(1)} all-to-all(f32[32,1,1024]{2,1,0:T(1,128)S(1)} %bitcast.47), channel_id=1, replica_groups=mesh['gx'=32,'gy'=16] {'gx'}, dimensions={0} | all-to-all | bytes 262144 | tf_op jit(solution)/shard_map/all_to_all | solution.py:393
  44.8 0.2 solve_gx.1
  44.9 17.3 %all_to_all.21 = f32[32,1,512]{2,1,0:T(1,128)S(1)} all-to-all(f32[32,1,512]{2,1,0:T(1,128)S(1)} %bitcast.43), channel_id=1, replica_groups=mesh['gx'=32,'gy'=16] {'gx'}, dimensions={0} | all-to-all | bytes 131072 | tf_op jit(solution)/shard_map/all_to_all | solution.py:393
  62.2 0.9 middle.1
  63.1 13.8 %all_to_all.22 = f32[16,1,2560]{2,1,0:T(1,128)S(1)} all-to-all(f32[16,1,2560]{2,1,0:T(1,128)S(1)} %bitcast.45), channel_id=1, replica_groups=mesh['gx'=32,'gy'=16] {'gy'}, dimensions={0} | all-to-all | bytes 327680 | tf_op jit(solution)/shard_map/all_to_all | solution.py:393
  76.9 0.1 solve_gy.1
  77.1 10.7 %all_to_all.23 = f32[16,1,1024]{2,1,0:T(1,128)S(1)} all-to-all(f32[16,1,1024]{2,1,0:T(1,128)S(1)} %bitcast.44), channel_id=1, replica_groups=mesh['gx'=32,'gy'=16] {'gy'}, dimensions={0} | all-to-all | bytes 131072 | tf_op jit(solution)/shard_map/all_to_all | solution.py:393
  87.8 1.1 %backward_y.1 = f32[32,4,16,128]{3,2,1,0:T(8,128)} custom-call(f32[128,128]{1,0:T(8,128)S(1)} %bitcast.42, f32[31,32,256]{2,1,0:T(8,128)S(1)} %get-tuple-element.28.phi_ref, f32[31,32,256]{2,1,0:T(8,128)S(1)} %get-tuple-element.29.gam_ref, f32[31,32,256]{2,1,0:T(8,128)S(1)} %get-tuple-element.30.tau_ref), custom_call_target="tpu_custom_call" | custom-call | flops 1048576 | bytes 1048576 | tf_op jit(solution)/shard_map/backward_y/pallas_call | solution.py:364
  (1 shorter events, 0.0 us)
Async XLA Ops:
  0.0 4.6 %copy-start = (f32[32,32,256]{2,1,0:T(8,128)S(1)}, f32[32,32,256]{2,1,0:T(8,128)}, u32[]{:S(2)}) copy-start(f32[32,32,256]{2,1,0:T(8,128)} %field_ref.3) | copy-start | bytes 3145732
  0.0 4.6 %copy-start.1 = (f32[32,32,256]{2,1,0:T(8,128)S(1)}, f32[32,32,256]{2,1,0:T(8,128)}, u32[]{:S(2)}) copy-start(f32[32,32,256]{2,1,0:T(8,128)} %weight_ref.3) | copy-start | bytes 3145732
  0.0 4.6 %copy-start.2 = (f32[32,32,256]{2,1,0:T(8,128)S(1)}, f32[32,32,256]{2,1,0:T(8,128)}, u32[]{:S(2)}) copy-start(f32[32,32,256]{2,1,0:T(8,128)} %c_ref.3) | copy-start | bytes 3145732
  1.1 8.8 %copy-start.3 = (f32[32,32,256]{2,1,0:T(8,128)S(1)}, f32[32,32,256]{2,1,0:T(8,128)}, u32[]{:S(2)}) copy-start(f32[32,32,256]{2,1,0:T(8,128)} %param.6) | copy-start | bytes 3145732
  1.1 10.9 %collective-permute-start.2 = (f32[256,1,128]{2,0,1:T(8,128)S(1)}, f32[256,1,128]{2,0,1:T(8,128)S(1)}, u32[]{:S(2)}, u32[]{:S(2)}) collective-permute-start(f32[256,1,128]{2,0,1:T(8,128)S(1)} %bitcast.46), channel_id=1, source_target_pairs={{0,1},{1,2},{2,3},{3,4},{4,5},{5,6},{6,7},{7,8},{8,9},{9,10},{10,1... | collective-permute-start | bytes 393224 | tf_op jit(solution)/shard_map/ppermute | solution.py:387
  5.1 11.9 %collective-permute-start = (f32[4,32,256]{2,1,0:T(8,128)S(1)}, f32[4,32,256]{2,1,0:T(8,128)S(1)}, u32[]{:S(2)}, u32[]{:S(2)}) collective-permute-start(f32[4,32,256]{2,1,0:T(8,128)S(1)} %get-tuple-element.18.up_ref), channel_id=1, source_target_pairs={{0,16},{16,32},{32,48},{48,64},{64,80},{80,96},{96,112},{112,128},... | collective-permute-start | bytes 393224 | tf_op jit(solution)/shard_map/ppermute | solution.py:387
  5.2 11.9 %collective-permute-start.1 = (f32[8,256]{1,0:T(8,128)S(1)}, f32[8,256]{1,0:T(8,128)S(1)}, u32[]{:S(2)}, u32[]{:S(2)}) collective-permute-start(f32[8,256]{1,0:T(8,128)S(1)} %get-tuple-element.19), channel_id=1, source_target_pairs={{0,17},{1,18},{2,19},{3,20},{4,21},{5,22},{6,23},{7,24},{8,25},{9,... | collective-permute-start | bytes 24584 | tf_op jit(solution)/shard_map/ppermute | solution.py:387
